TPU v7x, 256 devices: a whole 4x4x8 slice. The times are simulated.
256 devices in a mesh: lon: 64 (over x, y_hi, z), lat: 4 (over y_lo, core).
Axes of the slice: x: 4, y: 4 (y_hi: 2, y_lo: 2; y = y_hi * 2 + y_lo), z: 8, core: 2. Of those that a mesh axis runs over, the one named last changes fastest.
Arguments:
- first_block_input: bfloat16 [128, 2048, 192], P('lat', 'lon'), may hold values from -6 to 6
- first_block_preactivation: bfloat16 [128, 2048, 192], P('lat', 'lon'), may hold values from -8 to 8
- second_block_input: bfloat16 [128, 2048, 192], P('lat', 'lon'), may hold values from -6 to 6
- second_block_preactivation: bfloat16 [128, 2048, 192], P('lat', 'lon'), may hold values from -8 to 8
- output_gradient_final: bfloat16 [128, 2048, 192], P('lat', 'lon'), may hold values from -6 to 6
- first_block_conv_one: bfloat16 [9, 192, 192], replicated, may hold values from -0.15625 to 0.15625
- first_block_conv_two: bfloat16 [9, 192, 192], replicated, may hold values from -0.15625 to 0.15625
- second_block_conv_one: bfloat16 [9, 192, 192], replicated, may hold values from -0.15625 to 0.15625
- second_block_conv_two: bfloat16 [9, 192, 192], replicated, may hold values from -0.15625 to 0.15625
Outputs:
- first_block_input_gradient: bfloat16 [128, 2048, 192], P('lat', 'lon')
- first_block_conv_one_gradient: float32 [9, 192, 192], replicated
- first_block_conv_two_gradient: float32 [9, 192, 192], replicated
- second_block_conv_one_gradient: float32 [9, 192, 192], replicated
- second_block_conv_two_gradient: float32 [9, 192, 192], replicated
All inputs are finite; a program needn't handle non-finite values.
Results may differ from a plain program's by a relative error of at most 0.0061.
Values may be sent and summed in bfloat16 or wider, within the bound.
A program may use at most 128 MiB of HBM per device.

v0:
```python
import jax
import jax.numpy as jnp
from jax import lax
from jax.sharding import PartitionSpec as P

DILATION_FIRST = 16
DILATION_SECOND = 32


tap_offsets = [(row_tap, col_tap) for row_tap in (-1, 0, 1) for col_tap in (-1, 0, 1)]


def with_halo(block, sides, width, periodic):
    for axis, dim in sides:
        count = lax.axis_size(axis)
        forward = [(i, i + 1) for i in range(count - 1)]
        if periodic:
            forward.append((count - 1, 0))
        backward = [(target, source) for source, target in forward]
        low = lax.ppermute(
            lax.slice_in_dim(block, block.shape[dim] - width, None, axis=dim), axis, forward
        )
        high = lax.ppermute(lax.slice_in_dim(block, 0, width, axis=dim), axis, backward)
        block = jnp.concatenate([low, block, high], axis=dim)
    return block


def widen_active(values, dilation):
    across = with_halo(values, (("lon", 1),), dilation, True)
    return with_halo(across, (("lat", 0),), dilation, False)


def widen_gradient(values, dilation):
    across = with_halo(values, (("lon", 1),), dilation, True)
    return with_halo(across, (("lat", 0),), dilation, False)


def window(widened, row_shift, col_shift, dilation, height, breadth):
    top = dilation + row_shift * dilation
    left = dilation + col_shift * dilation
    return widened[top : top + height, left : left + breadth]


def weight_grad(widened, gradient, dilation):
    height, breadth = (gradient.shape[0], gradient.shape[1])
    return jnp.stack(
        [
            lax.dot_general(
                window(widened, row_tap, col_tap, dilation, height, breadth),
                gradient,
                (((0, 1), (0, 1)), ((), ())),
                preferred_element_type=jnp.float32,
            )
            for row_tap, col_tap in tap_offsets
        ]
    )


def pulled(gradient, widened, weights, dilation):
    height, breadth = (gradient.shape[0], gradient.shape[1])
    widened = widen_gradient(gradient, dilation)
    total = jnp.zeros(gradient.shape, jnp.float32)
    for row_index, row_tap in enumerate((-1, 0, 1)):
        joined = jnp.concatenate(
            [
                window(widened, -row_tap, -col_tap, dilation, height, breadth)
                for col_tap in (-1, 0, 1)
            ],
            2,
        )
        stacked = jnp.concatenate([weights[3 * row_index + col_index] for col_index in range(3)], 1)
        total = total + lax.dot_general(
            joined, stacked, (((2,), (1,)), ((), ())), preferred_element_type=jnp.float32
        )
    return total


def transpose_conv(gradient, weights, dilation):
    return pulled(gradient, None, weights, dilation)


def residual_block_backward(entry, hidden_pre, gradient, first, second, dilation):
    pre = hidden_pre.astype(jnp.float32)
    sigma = jax.nn.sigmoid(pre)
    hidden = (pre * sigma).astype(jnp.bfloat16)
    grad_second = weight_grad(widen_active(hidden, dilation), gradient, dilation)
    grad_hidden = transpose_conv(gradient, second, dilation)
    grad_pre = (grad_hidden * sigma * (1.0 + pre * (1.0 - sigma))).astype(jnp.bfloat16)
    grad_first = weight_grad(widen_active(entry, dilation), grad_pre, dilation)
    first_block_input_gradient = (
        gradient.astype(jnp.float32) + transpose_conv(grad_pre, first, dilation)
    ).astype(jnp.bfloat16)
    return (first_block_input_gradient, grad_first, grad_second)


def settle(first_grad, second_grad):
    return lax.psum((first_grad, second_grad), ("lon", "lat"))


def local(
    first_block_input,
    first_block_preactivation,
    second_block_input,
    second_block_preactivation,
    output_gradient_final,
    first_block_conv_one,
    first_block_conv_two,
    second_block_conv_one,
    second_block_conv_two,
):
    between_blocks_gradient, second_block_conv_one_gradient, second_block_conv_two_gradient = (
        residual_block_backward(
            second_block_input,
            second_block_preactivation,
            output_gradient_final,
            second_block_conv_one,
            second_block_conv_two,
            DILATION_SECOND,
        )
    )
    second_block_conv_one_gradient, second_block_conv_two_gradient = settle(
        second_block_conv_one_gradient, second_block_conv_two_gradient
    )
    first_block_input_gradient, first_block_conv_one_gradient, first_block_conv_two_gradient = (
        residual_block_backward(
            first_block_input,
            first_block_preactivation,
            between_blocks_gradient,
            first_block_conv_one,
            first_block_conv_two,
            DILATION_FIRST,
        )
    )
    first_block_conv_one_gradient, first_block_conv_two_gradient = settle(
        first_block_conv_one_gradient, first_block_conv_two_gradient
    )
    return (
        first_block_input_gradient,
        first_block_conv_one_gradient,
        first_block_conv_two_gradient,
        second_block_conv_one_gradient,
        second_block_conv_two_gradient,
    )


def solution(mesh):
    in_specs = (
        P("lat", "lon", None),
        P("lat", "lon", None),
        P("lat", "lon", None),
        P("lat", "lon", None),
        P("lat", "lon", None),
        P(),
        P(),
        P(),
        P(),
    )
    out_specs = (P("lat", "lon", None), P(), P(), P(), P())
    return jax.shard_map(local, mesh=mesh, in_specs=in_specs, out_specs=out_specs, check_vma=False)
```

profile of v0, /device:TPU:1, one launch (start us, length us, event | category | flops | bytes accessed | tf_op | source)
XLA Modules:
  0.0 508.3 jit_solution(3772339610091620265)
XLA Ops:
  7.2 2.5 collective-permute-start
  9.8 8.9 %collective-permute-start.1 = (bf16[32,32,192]{2,1,0:T(8,128)(2,1)}, bf16[32,32,192]{2,1,0:T(8,128)(2,1)S(1)}, u32[]{:S(2)}, u32[]{:S(2)}) collective-permute-start(bf16[32,32,192]{2,1,0:T(8,128)(2,1)} %param.13), channel_id=1, source_target_pairs={{4,0},{8,4},{12,8},{16,12},{20,16},{24,20},{28,24},{32,28},{36,32}... | collective-permute-start | bytes 1179656 | tf_op jit(solution)/shard_map/ppermute | solution.py:23
  19.8 7.2 %collective-permute-start.17 = (bf16[32,16,192]{2,1,0:T(8,128)(2,1)S(1)}, bf16[32,16,192]{2,1,0:T(8,128)(2,1)S(1)}, u32[]{:S(2)}, u32[]{:S(2)}) collective-permute-start(bf16[32,16,192]{2,1,0:T(8,128)(2,1)S(1)} %get-tuple-element.85), channel_id=1, source_target_pairs={{4,0},{8,4},{12,8},{16,12},{20,16},{24,20},{28,24},{32,28},{36,32}... | collective-permute-start | bytes 589832 | tf_op jit(solution)/shard_map/ppermute | solution.py:23
  29.9 6.1 %collective-permute-done.16 = bf16[32,16,192]{2,1,0:T(8,128)(2,1)S(1)} collective-permute-done((bf16[32,16,192]{2,1,0:T(8,128)(2,1)S(1)}, bf16[32,16,192]{2,1,0:T(8,128)(2,1)S(1)}, u32[]{:S(2)}, u32[]{:S(2)}) %collective-permute-start.16) | collective-permute-done | bytes 196640 | tf_op jit(solution)/shard_map/ppermute | solution.py:20
  36.3 4.3 collective-permute-done.21
  40.7 7.9 %collective-permute-start.25 = (bf16[32,32,192]{2,1,0:T(8,128)(2,1)S(1)}, bf16[32,32,192]{2,1,0:T(8,128)(2,1)S(1)}, u32[]{:S(2)}, u32[]{:S(2)}) collective-permute-start(bf16[32,32,192]{2,1,0:T(8,128)(2,1)S(1)} %copy-done.1), channel_id=1, source_target_pairs={{4,0},{8,4},{12,8},{16,12},{20,16},{24,20},{28,24},{32,28},{36,32}... | collective-permute-start | bytes 1179656 | tf_op jit(solution)/shard_map/ppermute | solution.py:23
  50.5 6.3 %collective-permute-start.3 = (bf16[32,96,192]{2,1,0:T(8,128)(2,1)S(1)}, bf16[32,96,192]{2,1,0:T(8,128)(2,1)S(1)}, u32[]{:S(2)}, u32[]{:S(2)}) collective-permute-start(bf16[32,96,192]{2,1,0:T(8,128)(2,1)S(1)} %constant_dynamic-update-slice_fusion), channel_id=1, source_target_pairs={{0,1},{1,2},{2,3},{4,5},{5,6},{6,7},{8,9},{9,10},{10,11},{12,13},{... | collective-permute-start | bytes 3538952 | tf_op jit(solution)/shard_map/ppermute | solution.py:20
  56.9 2.7 collective-permute-done.24
  59.5 5.8 %collective-permute-start.2 = (bf16[32,96,192]{2,1,0:T(8,128)(2,1)S(1)}, bf16[32,96,192]{2,1,0:T(8,128)(2,1)S(1)}, u32[]{:S(2)}, u32[]{:S(2)}) collective-permute-start(bf16[32,96,192]{2,1,0:T(8,128)(2,1)S(1)} %constant_dynamic-update-slice_fusion), channel_id=1, source_target_pairs={{1,0},{2,1},{3,2},{5,4},{6,5},{7,6},{9,8},{10,9},{11,10},{13,12},{... | collective-permute-start | bytes 3538952 | tf_op jit(solution)/shard_map/ppermute | solution.py:23
  67.4 2.2 collective-permute-done.29
  69.6 4.6 collective-permute-start.22
  77.2 12.1 %collective-permute-done.23 = bf16[16,64,192]{2,1,0:T(8,128)(2,1)S(1)} collective-permute-done((bf16[16,64,192]{2,1,0:T(8,128)(2,1)S(1)}, bf16[16,64,192]{2,1,0:T(8,128)(2,1)S(1)}, u32[]{:S(2)}, u32[]{:S(2)}) %collective-permute-start.23) | collective-permute-done | bytes 393248 | tf_op jit(solution)/shard_map/ppermute | solution.py:23
  91.2 4.1 collective-permute-start.26
  99.2 3.6 collective-permute-start.30
  103.9 8.3 %collective-permute-done.26 = bf16[32,96,192]{2,1,0:T(8,128)(2,1)S(1)} collective-permute-done((bf16[32,96,192]{2,1,0:T(8,128)(2,1)S(1)}, bf16[32,96,192]{2,1,0:T(8,128)(2,1)S(1)}, u32[]{:S(2)}, u32[]{:S(2)}) %collective-permute-start.26) | collective-permute-done | bytes 1179680 | tf_op jit(solution)/shard_map/ppermute | solution.py:20
  118.1 7.5 %collective-permute-start.5 = (bf16[32,32,192]{2,1,0:T(8,128)(2,1)S(1)}, bf16[32,32,192]{2,1,0:T(8,128)(2,1)S(1)}, u32[]{:S(2)}, u32[]{:S(2)}) collective-permute-start(bf16[32,32,192]{2,1,0:T(8,128)(2,1)S(1)} %fusion.95), channel_id=1, source_target_pairs={{4,0},{8,4},{12,8},{16,12},{20,16},{24,20},{28,24},{32,28},{36,32}... | collective-permute-start | bytes 1179656 | tf_op jit(solution)/shard_map/ppermute | solution.py:23
  126.3 8.3 %collective-permute-done.30 = bf16[32,96,192]{2,1,0:T(8,128)(2,1)S(1)} collective-permute-done((bf16[32,96,192]{2,1,0:T(8,128)(2,1)S(1)}, bf16[32,96,192]{2,1,0:T(8,128)(2,1)S(1)}, u32[]{:S(2)}, u32[]{:S(2)}) %collective-permute-start.30) | collective-permute-done | bytes 1179680 | tf_op jit(solution)/shard_map/ppermute | solution.py:20
  136.5 17.5 %collective-permute-done.4 = bf16[32,32,192]{2,1,0:T(8,128)(2,1)S(1)} collective-permute-done((bf16[32,32,192]{2,1,0:T(8,128)(2,1)S(1)}, bf16[32,32,192]{2,1,0:T(8,128)(2,1)S(1)}, u32[]{:S(2)}, u32[]{:S(2)}) %collective-permute-start.4) | collective-permute-done | bytes 393248 | tf_op jit(solution)/shard_map/ppermute | solution.py:20
  154.3 4.7 collective-permute-start.7
  164.1 15.1 %collective-permute-done.7 = bf16[32,96,192]{2,1,0:T(8,128)(2,1)S(1)} collective-permute-done((bf16[32,96,192]{2,1,0:T(8,128)(2,1)S(1)}, bf16[32,96,192]{2,1,0:T(8,128)(2,1)S(1)}, u32[]{:S(2)}, u32[]{:S(2)}) %collective-permute-start.7) | collective-permute-done | bytes 1179680 | tf_op jit(solution)/shard_map/ppermute | solution.py:20
  180.0 4.3 collective-permute-done.6
  185.3 7.2 %collective-permute-start.9 = (bf16[32,16,192]{2,1,0:T(8,128)(2,1)S(1)}, bf16[32,16,192]{2,1,0:T(8,128)(2,1)S(1)}, u32[]{:S(2)}, u32[]{:S(2)}) collective-permute-start(bf16[32,16,192]{2,1,0:T(8,128)(2,1)S(1)} %get-tuple-element.89), channel_id=1, source_target_pairs={{4,0},{8,4},{12,8},{16,12},{20,16},{24,20},{28,24},{32,28},{36,32}... | collective-permute-start | bytes 589832 | tf_op jit(solution)/shard_map/ppermute | solution.py:23
  196.5 2.9 collective-permute-start.11
  203.1 2.4 collective-permute-done.11
  205.5 4.4 collective-permute-done.10
  217.7 8.1 %collective-permute-start.13 = (bf16[32,16,192]{2,1,0:T(8,128)(2,1)S(1)}, bf16[32,16,192]{2,1,0:T(8,128)(2,1)S(1)}, u32[]{:S(2)}, u32[]{:S(2)}) collective-permute-start(bf16[32,16,192]{2,1,0:T(8,128)(2,1)S(1)} %get-tuple-element.87), channel_id=1, source_target_pairs={{4,0},{8,4},{12,8},{16,12},{20,16},{24,20},{28,24},{32,28},{36,32}... | collective-permute-start | bytes 589832 | tf_op jit(solution)/shard_map/ppermute | solution.py:23
  225.8 3.7 collective-permute-done.12
  232.7 2.4 collective-permute-start.14
  235.9 3.5 collective-permute-done.15
  239.4 5.2 %collective-permute-done.14 = bf16[16,64,192]{2,1,0:T(8,128)(2,1)S(1)} collective-permute-done((bf16[16,64,192]{2,1,0:T(8,128)(2,1)S(1)}, bf16[16,64,192]{2,1,0:T(8,128)(2,1)S(1)}, u32[]{:S(2)}, u32[]{:S(2)}) %collective-permute-start.14) | collective-permute-done | bytes 393248 | tf_op jit(solution)/shard_map/ppermute | solution.py:23
  248.4 244.5 %all-reduce.3.cloned.1.call-done = (f32[9,192,192]{2,1,0:T(8,128)}, f32[9,192,192]{2,1,0:T(8,128)}, f32[9,192,192]{2,1,0:T(8,128)}, f32[9,192,192]{2,1,0:T(8,128)}) async-done(((f32[9,192,192]{2,1,0:T(8,128)}, f32[9,192,192]{2,1,0:T(8,128)}, f32[9,192,192]{2,1,0:T(8,128)}, f32[9,192,192]{2,1,0:T(8,128)}), (f32[9,192,192]{2,1,0:T(8,128)}, f32[9,192,192]{2,1,0:T(8,128)}, f32[9,192,192]{2,1,0:T(8,128)}, ...) | async-done | bytes 5308432 | tf_op jit(solution)/shard_map/psum | solution.py:97
  492.9 2.9 copy.68
  (157 shorter events, 62.1 us)
Async XLA Ops:
  7.2 485.7 %all-reduce.3.cloned.1.call-start = ((), (), s32[]{:S(2)}) async-start(), calls=%async_computation | async-start | bytes 14155776 | tf_op jit(solution)/shard_map/psum | solution.py:97
  7.2 41.6 %collective-permute-start = (bf16[32,32,192]{2,1,0:T(8,128)(2,1)}, bf16[32,32,192]{2,1,0:T(8,128)(2,1)S(1)}, u32[]{:S(2)}, u32[]{:S(2)}) collective-permute-start(bf16[32,32,192]{2,1,0:T(8,128)(2,1)} %param.13), channel_id=1, source_target_pairs={{0,4},{4,8},{8,12},{12,16},{16,20},{20,24},{24,28},{28,32},{32,36}... | collective-permute-start | bytes 1179656 | tf_op jit(solution)/shard_map/ppermute | solution.py:20
  9.8 40.7 %collective-permute-start.1 = (bf16[32,32,192]{2,1,0:T(8,128)(2,1)}, bf16[32,32,192]{2,1,0:T(8,128)(2,1)S(1)}, u32[]{:S(2)}, u32[]{:S(2)}) collective-permute-start(bf16[32,32,192]{2,1,0:T(8,128)(2,1)} %param.13), channel_id=1, source_target_pairs={{4,0},{8,4},{12,8},{16,12},{20,16},{24,20},{28,24},{32,28},{36,32}... | collective-permute-start | bytes 1179656 | tf_op jit(solution)/shard_map/ppermute | solution.py:23
  19.7 16.3 %collective-permute-start.16 = (bf16[32,16,192]{2,1,0:T(8,128)(2,1)S(1)}, bf16[32,16,192]{2,1,0:T(8,128)(2,1)S(1)}, u32[]{:S(2)}, u32[]{:S(2)}) collective-permute-start(bf16[32,16,192]{2,1,0:T(8,128)(2,1)S(1)} %get-tuple-element.86), channel_id=1, source_target_pairs={{0,4},{4,8},{8,12},{12,16},{16,20},{20,24},{24,28},{28,32},{32,36}... | collective-permute-start | bytes 589832 | tf_op jit(solution)/shard_map/ppermute | solution.py:20
  19.8 16.3 %collective-permute-start.17 = (bf16[32,16,192]{2,1,0:T(8,128)(2,1)S(1)}, bf16[32,16,192]{2,1,0:T(8,128)(2,1)S(1)}, u32[]{:S(2)}, u32[]{:S(2)}) collective-permute-start(bf16[32,16,192]{2,1,0:T(8,128)(2,1)S(1)} %get-tuple-element.85), channel_id=1, source_target_pairs={{4,0},{8,4},{12,8},{16,12},{20,16},{24,20},{28,24},{32,28},{36,32}... | collective-permute-start | bytes 589832 | tf_op jit(solution)/shard_map/ppermute | solution.py:23
  28.4 12.3 %collective-permute-start.21 = (bf16[32,16,192]{2,1,0:T(8,128)(2,1)S(1)}, bf16[32,16,192]{2,1,0:T(8,128)(2,1)S(1)}, u32[]{:S(2)}, u32[]{:S(2)}) collective-permute-start(bf16[32,16,192]{2,1,0:T(8,128)(2,1)S(1)} %get-tuple-element.84), channel_id=1, source_target_pairs={{4,0},{8,4},{12,8},{16,12},{20,16},{24,20},{28,24},{32,28},{36,32}... | collective-permute-start | bytes 589832 | tf_op jit(solution)/shard_map/ppermute | solution.py:23
  36.0 12.6 %collective-permute-start.20 = (bf16[32,16,192]{2,1,0:T(8,128)(2,1)S(1)}, bf16[32,16,192]{2,1,0:T(8,128)(2,1)S(1)}, u32[]{:S(2)}, u32[]{:S(2)}) collective-permute-start(bf16[32,16,192]{2,1,0:T(8,128)(2,1)S(1)} %get-tuple-element.83), channel_id=1, source_target_pairs={{0,4},{4,8},{8,12},{12,16},{16,20},{20,24},{24,28},{28,32},{32,36}... | collective-permute-start | bytes 589832 | tf_op jit(solution)/shard_map/ppermute | solution.py:20
  36.1 23.5 %collective-permute-start.24 = (bf16[32,32,192]{2,1,0:T(8,128)(2,1)S(1)}, bf16[32,32,192]{2,1,0:T(8,128)(2,1)S(1)}, u32[]{:S(2)}, u32[]{:S(2)}) collective-permute-start(bf16[32,32,192]{2,1,0:T(8,128)(2,1)S(1)} %copy-done.1), channel_id=1, source_target_pairs={{0,4},{4,8},{8,12},{12,16},{16,20},{20,24},{24,28},{28,32},{32,36}... | collective-permute-start | bytes 1179656 | tf_op jit(solution)/shard_map/ppermute | solution.py:20
  40.7 24.8 %collective-permute-start.25 = (bf16[32,32,192]{2,1,0:T(8,128)(2,1)S(1)}, bf16[32,32,192]{2,1,0:T(8,128)(2,1)S(1)}, u32[]{:S(2)}, u32[]{:S(2)}) collective-permute-start(bf16[32,32,192]{2,1,0:T(8,128)(2,1)S(1)} %copy-done.1), channel_id=1, source_target_pairs={{4,0},{8,4},{12,8},{16,12},{20,16},{24,20},{28,24},{32,28},{36,32}... | collective-permute-start | bytes 1179656 | tf_op jit(solution)/shard_map/ppermute | solution.py:23
  48.6 21.0 %collective-permute-start.29 = (bf16[32,32,192]{2,1,0:T(8,128)(2,1)S(1)}, bf16[32,32,192]{2,1,0:T(8,128)(2,1)S(1)}, u32[]{:S(2)}, u32[]{:S(2)}) collective-permute-start(bf16[32,32,192]{2,1,0:T(8,128)(2,1)S(1)} %fusion.138), channel_id=1, source_target_pairs={{4,0},{8,4},{12,8},{16,12},{20,16},{24,20},{28,24},{32,28},{36,32}... | collective-permute-start | bytes 1179656 | tf_op jit(solution)/shard_map/ppermute | solution.py:23
  48.8 26.1 %collective-permute-start.28 = (bf16[32,32,192]{2,1,0:T(8,128)(2,1)S(1)}, bf16[32,32,192]{2,1,0:T(8,128)(2,1)S(1)}, u32[]{:S(2)}, u32[]{:S(2)}) collective-permute-start(bf16[32,32,192]{2,1,0:T(8,128)(2,1)S(1)} %fusion.138), channel_id=1, source_target_pairs={{0,4},{4,8},{8,12},{12,16},{16,20},{20,24},{24,28},{28,32},{32,36}... | collective-permute-start | bytes 1179656 | tf_op jit(solution)/shard_map/ppermute | solution.py:20
  50.5 45.9 %collective-permute-start.3 = (bf16[32,96,192]{2,1,0:T(8,128)(2,1)S(1)}, bf16[32,96,192]{2,1,0:T(8,128)(2,1)S(1)}, u32[]{:S(2)}, u32[]{:S(2)}) collective-permute-start(bf16[32,96,192]{2,1,0:T(8,128)(2,1)S(1)} %constant_dynamic-update-slice_fusion), channel_id=1, source_target_pairs={{0,1},{1,2},{2,3},{4,5},{5,6},{6,7},{8,9},{9,10},{10,11},{12,13},{... | collective-permute-start | bytes 3538952 | tf_op jit(solution)/shard_map/ppermute | solution.py:20
  59.5 39.6 %collective-permute-start.2 = (bf16[32,96,192]{2,1,0:T(8,128)(2,1)S(1)}, bf16[32,96,192]{2,1,0:T(8,128)(2,1)S(1)}, u32[]{:S(2)}, u32[]{:S(2)}) collective-permute-start(bf16[32,96,192]{2,1,0:T(8,128)(2,1)S(1)} %constant_dynamic-update-slice_fusion), channel_id=1, source_target_pairs={{1,0},{2,1},{3,2},{5,4},{6,5},{7,6},{9,8},{10,9},{11,10},{13,12},{... | collective-permute-start | bytes 3538952 | tf_op jit(solution)/shard_map/ppermute | solution.py:23
  65.5 23.8 %collective-permute-start.23 = (bf16[16,64,192]{2,1,0:T(8,128)(2,1)S(1)}, bf16[16,64,192]{2,1,0:T(8,128)(2,1)S(1)}, u32[]{:S(2)}, u32[]{:S(2)}) collective-permute-start(bf16[16,64,192]{2,1,0:T(8,128)(2,1)S(1)} %get-tuple-element.35), channel_id=1, source_target_pairs={{1,0},{2,1},{3,2},{5,4},{6,5},{7,6},{9,8},{10,9},{11,10},{13,12},{... | collective-permute-start | bytes 1179656 | tf_op jit(solution)/shard_map/ppermute | solution.py:23
  69.6 21.6 %collective-permute-start.22 = (bf16[16,64,192]{2,1,0:T(8,128)(2,1)S(1)}, bf16[16,64,192]{2,1,0:T(8,128)(2,1)S(1)}, u32[]{:S(2)}, u32[]{:S(2)}) collective-permute-start(bf16[16,64,192]{2,1,0:T(8,128)(2,1)S(1)} %get-tuple-element.36), channel_id=1, source_target_pairs={{0,1},{1,2},{2,3},{4,5},{5,6},{6,7},{8,9},{9,10},{10,11},{12,13},{... | collective-permute-start | bytes 1179656 | tf_op jit(solution)/shard_map/ppermute | solution.py:20
  74.9 138.1 %collective-permute-start.18 = (bf16[16,64,192]{2,1,0:T(8,128)(2,1)S(1)}, bf16[16,64,192]{2,1,0:T(8,128)(2,1)S(1)}, u32[]{:S(2)}, u32[]{:S(2)}) collective-permute-start(bf16[16,64,192]{2,1,0:T(8,128)(2,1)S(1)} %get-tuple-element.38), channel_id=1, source_target_pairs={{0,1},{1,2},{2,3},{4,5},{5,6},{6,7},{8,9},{9,10},{10,11},{12,13},{... | collective-permute-start | bytes 1179656 | tf_op jit(solution)/shard_map/ppermute | solution.py:20
  89.3 125.9 %collective-permute-start.19 = (bf16[16,64,192]{2,1,0:T(8,128)(2,1)S(1)}, bf16[16,64,192]{2,1,0:T(8,128)(2,1)S(1)}, u32[]{:S(2)}, u32[]{:S(2)}) collective-permute-start(bf16[16,64,192]{2,1,0:T(8,128)(2,1)S(1)} %get-tuple-element.37), channel_id=1, source_target_pairs={{1,0},{2,1},{3,2},{5,4},{6,5},{7,6},{9,8},{10,9},{11,10},{13,12},{... | collective-permute-start | bytes 1179656 | tf_op jit(solution)/shard_map/ppermute | solution.py:23
  91.2 21.0 %collective-permute-start.26 = (bf16[32,96,192]{2,1,0:T(8,128)(2,1)S(1)}, bf16[32,96,192]{2,1,0:T(8,128)(2,1)S(1)}, u32[]{:S(2)}, u32[]{:S(2)}) collective-permute-start(bf16[32,96,192]{2,1,0:T(8,128)(2,1)S(1)} %constant_dynamic-update-slice_fusion.6), channel_id=1, source_target_pairs={{0,1},{1,2},{2,3},{4,5},{5,6},{6,7},{8,9},{9,10},{10,11},{12,13},{... | collective-permute-start | bytes 3538952 | tf_op jit(solution)/shard_map/ppermute | solution.py:20
  96.4 21.7 %collective-permute-start.27 = (bf16[32,96,192]{2,1,0:T(8,128)(2,1)S(1)}, bf16[32,96,192]{2,1,0:T(8,128)(2,1)S(1)}, u32[]{:S(2)}, u32[]{:S(2)}) collective-permute-start(bf16[32,96,192]{2,1,0:T(8,128)(2,1)S(1)} %constant_dynamic-update-slice_fusion.6), channel_id=1, source_target_pairs={{1,0},{2,1},{3,2},{5,4},{6,5},{7,6},{9,8},{10,9},{11,10},{13,12},{... | collective-permute-start | bytes 3538952 | tf_op jit(solution)/shard_map/ppermute | solution.py:23
  99.2 35.5 %collective-permute-start.30 = (bf16[32,96,192]{2,1,0:T(8,128)(2,1)S(1)}, bf16[32,96,192]{2,1,0:T(8,128)(2,1)S(1)}, u32[]{:S(2)}, u32[]{:S(2)}) collective-permute-start(bf16[32,96,192]{2,1,0:T(8,128)(2,1)S(1)} %pad_maximum_fusion.4), channel_id=1, source_target_pairs={{0,1},{1,2},{2,3},{4,5},{5,6},{6,7},{8,9},{9,10},{10,11},{12,13},{... | collective-permute-start | bytes 3538952 | tf_op jit(solution)/shard_map/ppermute | solution.py:20
  112.2 49.6 %collective-permute-start.31 = (bf16[32,96,192]{2,1,0:T(8,128)(2,1)S(1)}, bf16[32,96,192]{2,1,0:T(8,128)(2,1)S(1)}, u32[]{:S(2)}, u32[]{:S(2)}) collective-permute-start(bf16[32,96,192]{2,1,0:T(8,128)(2,1)S(1)} %pad_maximum_fusion.4), channel_id=1, source_target_pairs={{1,0},{2,1},{3,2},{5,4},{6,5},{7,6},{9,8},{10,9},{11,10},{13,12},{... | collective-permute-start | bytes 3538952 | tf_op jit(solution)/shard_map/ppermute | solution.py:23
  118.1 18.4 %collective-permute-start.5 = (bf16[32,32,192]{2,1,0:T(8,128)(2,1)S(1)}, bf16[32,32,192]{2,1,0:T(8,128)(2,1)S(1)}, u32[]{:S(2)}, u32[]{:S(2)}) collective-permute-start(bf16[32,32,192]{2,1,0:T(8,128)(2,1)S(1)} %fusion.95), channel_id=1, source_target_pairs={{4,0},{8,4},{12,8},{16,12},{20,16},{24,20},{28,24},{32,28},{36,32}... | collective-permute-start | bytes 1179656 | tf_op jit(solution)/shard_map/ppermute | solution.py:23
  134.6 19.4 %collective-permute-start.4 = (bf16[32,32,192]{2,1,0:T(8,128)(2,1)S(1)}, bf16[32,32,192]{2,1,0:T(8,128)(2,1)S(1)}, u32[]{:S(2)}, u32[]{:S(2)}) collective-permute-start(bf16[32,32,192]{2,1,0:T(8,128)(2,1)S(1)} %fusion.95), channel_id=1, source_target_pairs={{0,4},{4,8},{8,12},{12,16},{16,20},{20,24},{24,28},{28,32},{32,36}... | collective-permute-start | bytes 1179656 | tf_op jit(solution)/shard_map/ppermute | solution.py:20
  154.3 24.8 %collective-permute-start.7 = (bf16[32,96,192]{2,1,0:T(8,128)(2,1)S(1)}, bf16[32,96,192]{2,1,0:T(8,128)(2,1)S(1)}, u32[]{:S(2)}, u32[]{:S(2)}) collective-permute-start(bf16[32,96,192]{2,1,0:T(8,128)(2,1)S(1)} %pad_maximum_fusion), channel_id=1, source_target_pairs={{0,1},{1,2},{2,3},{4,5},{5,6},{6,7},{8,9},{9,10},{10,11},{12,13},{... | collective-permute-start | bytes 3538952 | tf_op jit(solution)/shard_map/ppermute | solution.py:20
  159.7 24.5 %collective-permute-start.6 = (bf16[32,96,192]{2,1,0:T(8,128)(2,1)S(1)}, bf16[32,96,192]{2,1,0:T(8,128)(2,1)S(1)}, u32[]{:S(2)}, u32[]{:S(2)}) collective-permute-start(bf16[32,96,192]{2,1,0:T(8,128)(2,1)S(1)} %pad_maximum_fusion), channel_id=1, source_target_pairs={{1,0},{2,1},{3,2},{5,4},{6,5},{7,6},{9,8},{10,9},{11,10},{13,12},{... | collective-permute-start | bytes 3538952 | tf_op jit(solution)/shard_map/ppermute | solution.py:23
  185.2 11.0 %collective-permute-start.8 = (bf16[32,16,192]{2,1,0:T(8,128)(2,1)S(1)}, bf16[32,16,192]{2,1,0:T(8,128)(2,1)S(1)}, u32[]{:S(2)}, u32[]{:S(2)}) collective-permute-start(bf16[32,16,192]{2,1,0:T(8,128)(2,1)S(1)} %get-tuple-element.90), channel_id=1, source_target_pairs={{0,4},{4,8},{8,12},{12,16},{16,20},{20,24},{24,28},{28,32},{32,36}... | collective-permute-start | bytes 589832 | tf_op jit(solution)/shard_map/ppermute | solution.py:20
  185.3 10.9 %collective-permute-start.9 = (bf16[32,16,192]{2,1,0:T(8,128)(2,1)S(1)}, bf16[32,16,192]{2,1,0:T(8,128)(2,1)S(1)}, u32[]{:S(2)}, u32[]{:S(2)}) collective-permute-start(bf16[32,16,192]{2,1,0:T(8,128)(2,1)S(1)} %get-tuple-element.89), channel_id=1, source_target_pairs={{4,0},{8,4},{12,8},{16,12},{20,16},{24,20},{28,24},{32,28},{36,32}... | collective-permute-start | bytes 589832 | tf_op jit(solution)/shard_map/ppermute | solution.py:23
  196.5 9.0 %collective-permute-start.11 = (bf16[16,64,192]{2,1,0:T(8,128)(2,1)S(1)}, bf16[16,64,192]{2,1,0:T(8,128)(2,1)S(1)}, u32[]{:S(2)}, u32[]{:S(2)}) collective-permute-start(bf16[16,64,192]{2,1,0:T(8,128)(2,1)S(1)} %get-tuple-element.45), channel_id=1, source_target_pairs={{0,1},{1,2},{2,3},{4,5},{5,6},{6,7},{8,9},{9,10},{10,11},{12,13},{... | collective-permute-start | bytes 1179656 | tf_op jit(solution)/shard_map/ppermute | solution.py:20
  199.4 10.5 %collective-permute-start.10 = (bf16[16,64,192]{2,1,0:T(8,128)(2,1)S(1)}, bf16[16,64,192]{2,1,0:T(8,128)(2,1)S(1)}, u32[]{:S(2)}, u32[]{:S(2)}) collective-permute-start(bf16[16,64,192]{2,1,0:T(8,128)(2,1)S(1)} %get-tuple-element.46), channel_id=1, source_target_pairs={{1,0},{2,1},{3,2},{5,4},{6,5},{7,6},{9,8},{10,9},{11,10},{13,12},{... | collective-permute-start | bytes 1179656 | tf_op jit(solution)/shard_map/ppermute | solution.py:23
  217.6 11.9 %collective-permute-start.12 = (bf16[32,16,192]{2,1,0:T(8,128)(2,1)S(1)}, bf16[32,16,192]{2,1,0:T(8,128)(2,1)S(1)}, u32[]{:S(2)}, u32[]{:S(2)}) collective-permute-start(bf16[32,16,192]{2,1,0:T(8,128)(2,1)S(1)} %get-tuple-element.88), channel_id=1, source_target_pairs={{0,4},{4,8},{8,12},{12,16},{16,20},{20,24},{24,28},{28,32},{32,36}... | collective-permute-start | bytes 589832 | tf_op jit(solution)/shard_map/ppermute | solution.py:20
  217.7 12.7 %collective-permute-start.13 = (bf16[32,16,192]{2,1,0:T(8,128)(2,1)S(1)}, bf16[32,16,192]{2,1,0:T(8,128)(2,1)S(1)}, u32[]{:S(2)}, u32[]{:S(2)}) collective-permute-start(bf16[32,16,192]{2,1,0:T(8,128)(2,1)S(1)} %get-tuple-element.87), channel_id=1, source_target_pairs={{4,0},{8,4},{12,8},{16,12},{20,16},{24,20},{28,24},{32,28},{36,32}... | collective-permute-start | bytes 589832 | tf_op jit(solution)/shard_map/ppermute | solution.py:23
  232.7 11.9 %collective-permute-start.14 = (bf16[16,64,192]{2,1,0:T(8,128)(2,1)S(1)}, bf16[16,64,192]{2,1,0:T(8,128)(2,1)S(1)}, u32[]{:S(2)}, u32[]{:S(2)}) collective-permute-start(bf16[16,64,192]{2,1,0:T(8,128)(2,1)S(1)} %get-tuple-element.42), channel_id=1, source_target_pairs={{1,0},{2,1},{3,2},{5,4},{6,5},{7,6},{9,8},{10,9},{11,10},{13,12},{... | collective-permute-start | bytes 1179656 | tf_op jit(solution)/shard_map/ppermute | solution.py:23
  (17 other events, 100.2 us)
Sparse Core Ops, SparseCore 0:
  217.7 275.1 all-reduce.2
where the time goes:
time: 518 us; the launch traced here: 508 us
  waiting for transfers between devices  347 us (67%)
  starting transfers between devices  101 us (19%)
  matrix products  22.3 us (4%)
  local copies, waits for them, and re-layouts  15.7 us (3%)
  between operations  15.3 us (3%)
  other arithmetic  6.13 us (1%)
    psum x1, waiting for transfers between devices, settle(): return lax.psum((first_grad, second_grad), ('lon', 'lat'))  244 us
    ppermute x16, waiting for transfers between devices, with_halo(): lax.ppermute(lax.slice_in_dim(block, block.shape[dim] - width, None, axis...  67.5 us
    ppermute x16, starting transfers between devices, with_halo(): lax.ppermute(lax.slice_in_dim(block, 0, width, axis=dim), axis, backward)  67 us
    ppermute x16, waiting for transfers between devices, with_halo(): lax.ppermute(lax.slice_in_dim(block, 0, width, axis=dim), axis, backward)  35.4 us
    ppermute x16, starting transfers between devices, with_halo(): lax.ppermute(lax.slice_in_dim(block, block.shape[dim] - width, None, axis...  34.4 us
    dot_general x36, matrix products, weight_grad(): lax.dot_general(window(widened, row_tap, col_tap, dilation, height, bread...  12.7 us
    unnamed x42, local copies, waits for them, and re-layouts  12.3 us
  transfers between devices with their start and end apart: 33, of which 19 were waited for; matrix products, arithmetic and copies ran while one was open for 6% of the time, Pallas kernels for 0%

commit v1 on v0

v1 whole, which is shorter than its diff:
```python
import jax
import jax.numpy as jnp
from jax import lax
from jax.experimental import pallas as pl
from jax.experimental.pallas import tpu as pltpu
from jax.sharding import PartitionSpec as P

C = 192
DILATION_FIRST = 16
DILATION_SECOND = 32
MESH = pl.DeviceIdType.MESH
BF = jnp.bfloat16
F32 = jnp.float32
T = 32
ROWS = 3072
HALF, QUART, SHARD = ROWS // 2, ROWS // 8, ROWS // 32


class Place:
    def __init__(self):
        lon, lat = lax.axis_index("lon"), lax.axis_index("lat")
        self.lon, self.lat = lon, lat
        self.x, self.yh, self.z = lon // 16, (lon // 8) % 2, lon % 8
        self.yl, self.core = lat // 2, lat % 2
        self.y = self.yh * 2 + self.yl
        self.east = {"lon": (lon + 1) % 64, "lat": lat}
        self.west = {"lon": (lon + 63) % 64, "lat": lat}
        self.north = {"lon": lon, "lat": jnp.minimum(lat + 1, 3)}
        self.south = {"lon": lon, "lat": jnp.maximum(lat - 1, 0)}
        self.twin = {"lon": lon, "lat": lat + 1 - 2 * self.core}
        self.has_north, self.has_south = lat < 3, lat > 0

    def at_x(self, k):
        x = (self.x + k) % 4
        return x, {"lon": x * 16 + self.lon % 16, "lat": self.lat}

    def at_y(self, k):
        y = (self.y + k) % 4
        lon = self.x * 16 + (y // 2) * 8 + self.z
        return y, {"lon": lon, "lat": (y % 2) * 2 + self.core}

    def at_z(self, k):
        z = (self.z + k) % 8
        return z, {"lon": self.lon - self.z + z, "lat": self.lat}


def remote(src, dst, send, recv, where):
    return pltpu.make_async_remote_copy(
        src_ref=src, dst_ref=dst, send_sem=send, recv_sem=recv, device_id=where, device_id_type=MESH
    )


class Sems:
    def __init__(self, send, recv):
        self.send, self.recv, self.n = send, recv, 0

    def take(self):
        k = self.n
        self.n += 1
        return self.send.at[k], self.recv.at[k]


class Reduction:
    def __init__(self, place, sems, local, from_twin, xs, xr, ys, yr, zs, zr, out):
        self.p, self.local, self.from_twin = place, local, from_twin
        self.xs, self.xr, self.ys, self.yr, self.zs, self.zr, self.out = xs, xr, ys, yr, zs, zr, out
        p = place
        other = pl.multiple_of((1 - p.core) * HALF, HALF)
        mine = pl.multiple_of(p.core * HALF, HALF)
        xo = pl.multiple_of(mine + p.x * QUART, QUART)
        yo = pl.multiple_of(xo + p.y * SHARD, SHARD)
        self.mine, self.xo, self.yo = mine, xo, yo
        self.twin = [remote(local.at[pl.ds(other, HALF)], from_twin, *sems.take(), p.twin)]
        self.to_x = []
        for k in (1, 2, 3):
            x, where = p.at_x(k)
            src = xs.at[pl.ds(pl.multiple_of(x * QUART, QUART), QUART)]
            self.to_x.append(remote(src, xr.at[k - 1], *sems.take(), where))
        self.to_y = []
        for k in (1, 2, 3):
            y, where = p.at_y(k)
            src = ys.at[pl.ds(pl.multiple_of(y * SHARD, SHARD), SHARD)]
            self.to_y.append(remote(src, yr.at[k - 1], *sems.take(), where))
        self.to_z = [remote(zs, zr.at[p.z], *sems.take(), p.at_z(k)[1]) for k in range(1, 8)]
        ref = out.at[pl.ds(yo, SHARD)]
        self.all_y = [remote(ref, ref, *sems.take(), p.at_y(k)[1]) for k in (1, 2, 3)]
        ref = out.at[pl.ds(xo, QUART)]
        self.all_x = [remote(ref, ref, *sems.take(), p.at_x(k)[1]) for k in (1, 2, 3)]
        ref = out.at[pl.ds(mine, HALF)]
        self.all_twin = [remote(ref, ref, *sems.take(), p.twin)]
        self.step = 0

    def go(self):
        getattr(self, f"step{self.step}")()
        self.step += 1

    def start(self, copies):
        for copy in copies:
            copy.start()

    def arrive(self, copies):
        for copy in copies:
            copy.wait_recv()

    def step0(self):
        self.start(self.twin)

    def step1(self):
        self.arrive(self.twin)

        @pl.loop(0, HALF // 128)
        def _(i):
            rows = pl.ds(pl.multiple_of(i * 128, 128), 128)
            own = self.local[pl.ds(pl.multiple_of(self.mine + i * 128, 128), 128)]
            self.xs[rows] = (own + self.from_twin[rows]).astype(BF)

        self.start(self.to_x)

    def step2(self):
        self.arrive(self.to_x)
        base = pl.multiple_of(self.p.x * QUART, QUART)
        total = self.xs[pl.ds(base, QUART)].astype(F32)
        for k in range(3):
            total = total + self.xr[k].astype(F32)
        self.ys[...] = total
        self.start(self.to_y)

    def step3(self):
        self.arrive(self.to_y)
        total = self.ys[pl.ds(pl.multiple_of(self.p.y * SHARD, SHARD), SHARD)]
        for k in range(3):
            total = total + self.yr[k]
        total = total.astype(BF)
        self.zs[...] = total
        self.zr[self.p.z] = total
        self.start(self.to_z)

    def step4(self):
        self.arrive(self.to_z)
        total = self.zr[0].astype(F32)
        for k in range(1, 8):
            total = total + self.zr[k].astype(F32)
        self.out[pl.ds(self.yo, SHARD)] = total.astype(BF)
        self.start(self.all_y)

    def step5(self):
        self.arrive(self.all_y)
        self.start(self.all_x)

    def step6(self):
        self.arrive(self.all_x)
        self.start(self.all_twin)

    def step7(self):
        self.arrive(self.all_twin)

    def drain(self):
        for copies in (self.twin, self.to_x, self.to_y, self.to_z, self.all_y, self.all_x, self.all_twin):
            for copy in copies:
                copy.wait_send()


def pack_rows(v, half):
    return jnp.concatenate([v[:half, :, 128:], v[half:, :, 128:]], axis=-1)


class LonHalo:
    def __init__(self, place, sems, tile, packed, plus, minus, got_plus, got_minus, d):
        self.tile, self.packed, self.plus, self.minus, self.d = tile, packed, plus, minus, d
        self.got_plus, self.got_minus = got_plus, got_minus
        low, high = pl.ds(0, d), pl.ds(T - d, d)
        wide = pl.ds(0, 128)
        self.copies = [
            remote(tile.at[:, high, wide], plus.at[:, low, wide], *sems.take(), place.east),
            remote(tile.at[:, low, wide], minus.at[:, high, wide], *sems.take(), place.west),
            remote(packed.at[:, high], got_plus, *sems.take(), place.east),
            remote(packed.at[:, low], got_minus, *sems.take(), place.west),
        ]

    def start(self):
        for copy in self.copies[:2]:
            copy.start()
        self.packed[...] = pack_rows(self.tile[...], T // 2)
        for copy in self.copies[2:]:
            copy.start()
        d = self.d
        if d < T:
            self.plus[:, d:, :] = self.tile[:, : T - d, :]
            self.minus[:, : T - d, :] = self.tile[:, d:, :]

    def arrive(self):
        for copy in self.copies:
            copy.wait_recv()
        d, h = self.d, T // 2
        self.plus[:h, :d, 128:] = self.got_plus[:, :, :64]
        self.plus[h:, :d, 128:] = self.got_plus[:, :, 64:]
        self.minus[:h, T - d :, 128:] = self.got_minus[:, :, :64]
        self.minus[h:, T - d :, 128:] = self.got_minus[:, :, 64:]

    def drain(self):
        for copy in self.copies:
            copy.wait_send()


def pack_columns(v):
    return jnp.concatenate([v[:, : T // 2, 128:], v[:, T // 2 :, 128:]], axis=-1)


class LatPair:
    def __init__(self, place, copies_north, copies_south):
        self.p, self.to_north, self.to_south = place, copies_north, copies_south

    def start(self):
        @pl.when(self.p.has_north)
        def _():
            for copy in self.to_north:
                copy.start()

        @pl.when(self.p.has_south)
        def _():
            for copy in self.to_south:
                copy.start()

    def arrive(self):
        @pl.when(self.p.has_south)
        def _():
            for copy in self.to_north:
                copy.wait_recv()

        @pl.when(self.p.has_north)
        def _():
            for copy in self.to_south:
                copy.wait_recv()

    def drain(self):
        @pl.when(self.p.has_north)
        def _():
            for copy in self.to_north:
                copy.wait_send()

        @pl.when(self.p.has_south)
        def _():
            for copy in self.to_south:
                copy.wait_send()


class Activation:
    def __init__(self, place, sems, wide, packed, got, turned, d):
        self.p, self.wide, self.packed, self.got, self.turned, self.d = place, wide, packed, got, turned, d
        lanes = pl.ds(0, 128)
        top, bottom = pl.ds(d, d), pl.ds(T, d)
        self.halo = LatPair(
            place,
            [
                remote(wide.at[bottom, :, lanes], wide.at[pl.ds(0, d), :, lanes], *sems.take(), place.north),
                remote(packed.at[pl.ds(T - d, d)], got.at[0], *sems.take(), place.north),
            ],
            [
                remote(wide.at[top, :, lanes], wide.at[pl.ds(T + d, d), :, lanes], *sems.take(), place.south),
                remote(packed.at[pl.ds(0, d)], got.at[1], *sems.take(), place.south),
            ],
        )

    def start(self):
        d = self.d

        @pl.loop(0, 4)
        def _(i):
            v = self.wide[pl.ds(d + i * 8, 8)]
            self.packed[pl.ds(i * 8, 8)] = pack_columns(v)

        self.halo.start()

        @pl.when(jnp.logical_not(self.p.has_south))
        def _():
            self.wide[:d] = jnp.zeros((d, T, C), BF)

        @pl.when(jnp.logical_not(self.p.has_north))
        def _():
            self.wide[T + d :] = jnp.zeros((d, T, C), BF)

    def arrive(self):
        d, h = self.d, T // 2
        self.halo.arrive()

        @pl.when(self.p.has_south)
        def _():
            self.wide[:d, :h, 128:] = self.got[0, :, :, :64]
            self.wide[:d, h:, 128:] = self.got[0, :, :, 64:]

        @pl.when(self.p.has_north)
        def _():
            self.wide[T + d :, :h, 128:] = self.got[1, :, :, :64]
            self.wide[T + d :, h:, 128:] = self.got[1, :, :, 64:]

        @pl.loop(0, (T + 2 * d) // 8)
        def _(i):
            v = self.wide[pl.ds(i * 8, 8)].reshape(8 * T, C)
            self.turned[:, pl.ds(pl.multiple_of(i * 8 * T, 8 * T), 8 * T)] = v.T

    def weight_gradient(self, minus, tile, plus, into):
        cells = T * T

        @pl.loop(0, 3)
        def _(r):
            start = pl.multiple_of(r * self.d * T, 512)
            turned = self.turned[:, pl.ds(start, cells)]
            for c, g in enumerate((minus, tile, plus)):
                d = jnp.dot(turned, g[...].reshape(cells, C), preferred_element_type=F32)
                base = pl.multiple_of((3 * r + c) * 288, 32)
                into[pl.ds(base, C)] = d[:, :128]
                into[pl.ds(base + C, C // 2)] = jnp.concatenate([d[: C // 2, 128:], d[C // 2 :, 128:]], axis=1)

        into[9 * 288 :] = jnp.zeros((ROWS - 9 * 288, 128), F32)


class Pull:
    def __init__(self, place, sems, minus, tile, plus, weights, wide_out, packed_out, wide_in, packed_in, total, d):
        self.p, self.g, self.w, self.d = place, (minus, tile, plus), weights, d
        self.wide_out, self.packed_out, self.wide_in, self.packed_in = wide_out, packed_out, wide_in, packed_in
        self.total = total
        self.halo = LatPair(
            place,
            [
                remote(wide_out.at[0], wide_in.at[0], *sems.take(), place.north),
                remote(packed_out.at[0], packed_in.at[0], *sems.take(), place.north),
            ],
            [
                remote(wide_out.at[1], wide_in.at[1], *sems.take(), place.south),
                remote(packed_out.at[1], packed_in.at[1], *sems.take(), place.south),
            ],
        )

    def partial(self, r, row):
        total = None
        for c in range(3):
            g = self.g[c][pl.ds(row, 8)].reshape(8 * T, C)
            term = lax.dot_general(
                g, self.w[3 * (r + 1) + c], (((1,), (1,)), ((), ())), preferred_element_type=F32
            )
            total = term if total is None else total + term
        return total.reshape(8, T, C)

    def send(self):
        d = self.d

        @pl.loop(0, d // 8)
        def _(i):
            for slot, r, first in ((0, 1, T - d), (1, -1, 0)):
                v = self.partial(r, first + i * 8).astype(BF)
                self.wide_out[slot, pl.ds(i * 8, 8)] = v[:, :, :128]
                self.packed_out[slot, pl.ds(i * 8, 8)] = pack_columns(v)

        self.halo.start()

        @pl.when(jnp.logical_not(self.p.has_south))
        def _():
            self.wide_in[0] = jnp.zeros(self.wide_in.shape[1:], BF)
            self.packed_in[0] = jnp.zeros(self.packed_in.shape[1:], BF)

        @pl.when(jnp.logical_not(self.p.has_north))
        def _():
            self.wide_in[1] = jnp.zeros(self.wide_in.shape[1:], BF)
            self.packed_in[1] = jnp.zeros(self.packed_in.shape[1:], BF)

    def stay(self):
        d = self.d

        @pl.loop(0, T // 8)
        def _(i):
            self.total[pl.ds(i * 8, 8)] = self.partial(0, i * 8)

        if d < T:

            @pl.loop(0, (T - d) // 8)
            def _(i):
                self.total[pl.ds(d + i * 8, 8)] += self.partial(1, i * 8)
                self.total[pl.ds(i * 8, 8)] += self.partial(-1, d + i * 8)

    def finish(self, use):
        d = self.d
        self.halo.arrive()

        def got(slot, row):
            w = self.wide_in[slot, pl.ds(row, 8)].astype(F32)
            q = self.packed_in[slot, pl.ds(row, 8)].astype(F32)
            return jnp.concatenate([w, jnp.concatenate([q[:, :, :64], q[:, :, 64:]], axis=1)], axis=-1)

        if d == T:

            @pl.loop(0, T // 8)
            def _(i):
                use(i * 8, self.total[pl.ds(i * 8, 8)] + got(0, i * 8) + got(1, i * 8))

        else:

            @pl.loop(0, d // 8)
            def _(i):
                use(i * 8, self.total[pl.ds(i * 8, 8)] + got(0, i * 8))
                use(T - d + i * 8, self.total[pl.ds(T - d + i * 8, 8)] + got(1, i * 8))


def scratch():
    v = pltpu.VMEM
    shapes = {}
    for b, d in (("1", DILATION_FIRST), ("2", DILATION_SECOND)):
        shapes["a" + b] = v((T, T, C), BF)
        shapes["slope" + b] = v((T, T, C), F32)
        for n in ("w1", "w2"):
            shapes[n + b] = v((9, C, C), BF)
        for n in ("h", "x"):
            shapes[n + b] = v((T + 2 * d, T, C), BF)
            shapes[n + b + "packed"] = v((T, T // 2, 128), BF)
            shapes[n + b + "got"] = v((2, d, T // 2, 128), BF)
            shapes[n + b + "turned"] = v((C, (T + 2 * d) * T), BF)
        for n in ("g", "q"):
            shapes[n + b] = v((T, T, C), BF)
            shapes[n + b + "packed"] = v((T // 2, T, 128), BF)
            for s in ("plus", "minus"):
                shapes[n + b + s] = v((T, T, C), BF)
                shapes[n + b + "got_" + s] = v((T // 2, d, 128), BF)
            for s in ("wide_out", "wide_in"):
                shapes[n + b + s] = v((2, d, T, 128), BF)
            for s in ("packed_out", "packed_in"):
                shapes[n + b + s] = v((2, d, T // 2, 128), BF)
        for n in ("1", "2"):
            m = "r" + n + b
            shapes[m + "local"] = v((ROWS, 128), F32)
            shapes[m + "from_twin"] = v((HALF, 128), F32)
            shapes[m + "xs"] = v((HALF, 128), BF)
            shapes[m + "xr"] = v((3, QUART, 128), BF)
            shapes[m + "ys"] = v((QUART, 128), F32)
            shapes[m + "yr"] = v((3, SHARD, 128), F32)
            shapes[m + "zs"] = v((SHARD, 128), BF)
            shapes[m + "zr"] = v((8, SHARD, 128), BF)
            shapes[m + "out"] = v((ROWS, 128), BF)
    shapes["total"] = v((T, T, C), F32)
    shapes["dx"] = v((T, T, C), BF)
    shapes["load"] = pltpu.SemaphoreType.DMA((9,))
    shapes["store"] = pltpu.SemaphoreType.DMA((5,))
    shapes["send"] = pltpu.SemaphoreType.DMA((160,))
    shapes["recv"] = pltpu.SemaphoreType.DMA((160,))
    return shapes


NAMES = tuple(scratch())


def body(x1, a1, x2, a2, g2, w11, w21, w12, w22, dx_out, r11_out, r21_out, r12_out, r22_out, *refs):
    s = dict(zip(NAMES, refs))
    p = Place()
    loads = {}
    d1, d2 = DILATION_FIRST, DILATION_SECOND
    for k, (name, src, dst) in enumerate(
        (
            ("g2", g2, s["g2"]),
            ("a2", a2, s["a2"]),
            ("x2", x2, s["x2"].at[pl.ds(d2, T)]),
            ("w22", w22, s["w22"]),
            ("a1", a1, s["a1"]),
            ("x1", x1, s["x1"].at[pl.ds(d1, T)]),
            ("w12", w12, s["w12"]),
            ("w21", w21, s["w21"]),
            ("w11", w11, s["w11"]),
        )
    ):
        loads[name] = pltpu.make_async_copy(src, dst, s["load"].at[k])
        loads[name].start()

    barrier = pltpu.get_barrier_semaphore()
    peers = [p.east, p.west, p.twin]
    peers += [p.at_x(k)[1] for k in (1, 2, 3)] + [p.at_y(k)[1] for k in (1, 2, 3)]
    peers += [p.at_z(k)[1] for k in range(1, 8)]
    for where in peers:
        pl.semaphore_signal(barrier, inc=1, device_id=where, device_id_type=MESH)
    for cond, where in ((p.has_north, p.north), (p.has_south, p.south)):

        @pl.when(cond)
        def _():
            pl.semaphore_signal(barrier, inc=1, device_id=where, device_id_type=MESH)

    expected = len(peers) + p.has_north.astype(jnp.int32) + p.has_south.astype(jnp.int32)

    sems = Sems(s["send"], s["recv"])

    def reduction(m):
        names = ("local", "from_twin", "xs", "xr", "ys", "yr", "zs", "zr", "out")
        return Reduction(p, sems, *(s[m + n] for n in names))

    def lon_halo(m, d):
        names = ("", "packed", "plus", "minus", "got_plus", "got_minus")
        return LonHalo(p, sems, *(s[m + n] for n in names), d)

    def pull(m, w, d):
        names = ("minus", "", "plus")
        outs = ("wide_out", "packed_out", "wide_in", "packed_in")
        return Pull(p, sems, *(s[m + n] for n in names), s[w], *(s[m + n] for n in outs), s["total"], d)

    def activation(m, d):
        return Activation(p, sems, *(s[m + n] for n in ("", "packed", "got", "turned")), d)

    red = {m: reduction(m) for m in ("r22", "r12", "r21", "r11")}
    halos = {m: lon_halo(m, d) for m, d in (("g2", d2), ("q2", d2), ("g1", d1), ("q1", d1))}
    pulls = {
        m: pull(m, w, d) for m, w, d in (("g2", "w22", d2), ("q2", "w12", d2), ("g1", "w21", d1), ("q1", "w11", d1))
    }
    acts = {m: activation(m, d) for m, d in (("h2", d2), ("x2", d2), ("h1", d1), ("x1", d1))}

    def gate(b, d):
        @pl.loop(0, T // 4)
        def _(i):
            rows = pl.ds(i * 4, 4)
            pre = s["a" + b][rows].astype(F32)
            sigma = jax.nn.sigmoid(pre)
            s["h" + b][pl.ds(d + i * 4, 4)] = (pre * sigma).astype(BF)
            s["slope" + b][rows] = sigma * (1.0 + pre * (1.0 - sigma))

    def use_pre(b):
        def use(row, v):
            s["q" + b][pl.ds(row, 8)] = (v * s["slope" + b][pl.ds(row, 8)]).astype(BF)

        return use

    def use_x(b, into):
        def use(row, v):
            into[pl.ds(row, 8)] = (s["g" + b][pl.ds(row, 8)].astype(F32) + v).astype(BF)

        return use

    def weight(act, m, r):
        acts[act].weight_gradient(s[m + "minus"], s[m], s[m + "plus"], s[r + "local"])

    loads["g2"].wait()
    pl.semaphore_wait(barrier, expected)
    halos["g2"].start()
    loads["a2"].wait()
    gate("2", d2)
    acts["h2"].start()
    loads["x2"].wait()
    acts["x2"].start()
    loads["a1"].wait()
    gate("1", d1)
    acts["h1"].start()
    loads["x1"].wait()
    acts["x1"].start()
    acts["h2"].arrive()
    for name in ("w22", "w12", "w21", "w11"):
        loads[name].wait()

    halos["g2"].arrive()
    pulls["g2"].send()
    pulls["g2"].stay()
    weight("h2", "g2", "r22")
    red["r22"].go()
    acts["x2"].arrive()
    pulls["g2"].finish(use_pre("2"))
    halos["q2"].start()
    red["r22"].go()
    acts["h1"].arrive()
    acts["x1"].arrive()
    red["r22"].go()

    halos["q2"].arrive()
    pulls["q2"].send()
    pulls["q2"].stay()
    weight("x2", "q2", "r12")
    red["r12"].go()
    red["r22"].go()
    pulls["q2"].finish(use_x("2", s["g1"]))
    halos["g1"].start()
    red["r12"].go()
    red["r22"].go()

    halos["g1"].arrive()
    pulls["g1"].send()
    pulls["g1"].stay()
    weight("h1", "g1", "r21")
    red["r21"].go()
    red["r12"].go()
    red["r22"].go()
    pulls["g1"].finish(use_pre("1"))
    halos["q1"].start()
    red["r21"].go()
    red["r12"].go()
    red["r22"].go()

    halos["q1"].arrive()
    weight("x1", "q1", "r11")
    red["r11"].go()
    pulls["q1"].send()
    pulls["q1"].stay()
    red["r11"].go()
    red["r21"].go()
    red["r12"].go()
    pulls["q1"].finish(use_x("1", s["dx"]))
    stores = [pltpu.make_async_copy(s["dx"], dx_out, s["store"].at[0])]
    stores[0].start()
    red["r22"].go()
    red["r11"].go()
    red["r21"].go()
    red["r12"].go()
    red["r11"].go()
    red["r21"].go()
    red["r12"].go()
    red["r11"].go()
    red["r21"].go()
    red["r12"].go()
    red["r11"].go()
    red["r21"].go()
    red["r11"].go()
    red["r21"].go()
    red["r11"].go()
    for k, (m, out) in enumerate((("r22", r22_out), ("r12", r12_out), ("r21", r21_out), ("r11", r11_out))):
        stores.append(pltpu.make_async_copy(s[m + "out"], out, s["store"].at[1 + k]))
        stores[-1].start()
    for part in (*halos.values(), *red.values()):
        part.drain()
    for part in (*pulls.values(), *acts.values()):
        part.halo.drain()
    for copy in stores:
        copy.wait()


def unpack(packed):
    taps = packed[: 9 * 288].reshape(9, 288, 128)
    rest = taps[:, C:].reshape(9, C // 2, 2, 64).transpose(0, 2, 1, 3).reshape(9, C, 64)
    return jnp.concatenate([taps[:, :C], rest], axis=-1).astype(F32)


def local(x1, a1, x2, a2, g2, w11, w21, w12, w22):
    shapes = scratch()
    anywhere = pl.BlockSpec(memory_space=pl.ANY)
    packed = jax.ShapeDtypeStruct((ROWS, 128), BF)
    dx, *sums = pl.pallas_call(
        body,
        name="backward",
        out_shape=(jax.ShapeDtypeStruct((T, T, C), BF), packed, packed, packed, packed),
        in_specs=[anywhere] * 9,
        out_specs=[anywhere] * 5,
        scratch_shapes=list(shapes.values()),
        compiler_params=pltpu.CompilerParams(
            collective_id=0, has_side_effects=True, vmem_limit_bytes=60 * 1024 * 1024
        ),
    )(x1, a1, x2, a2, g2, w11, w21, w12, w22)
    return (dx, *(unpack(v) for v in sums))


def solution(mesh):
    tile = P("lat", "lon", None)
    return jax.shard_map(
        local,
        mesh=mesh,
        in_specs=(tile,) * 5 + (P(),) * 4,
        out_specs=(tile, P(), P(), P(), P()),
        check_vma=False,
    )
```

time: 518 us -> 140 us (0.27); the launches traced: 508 us -> 139 us
  waiting for transfers between devices: 347 us -> 0 us
  Pallas kernels: 0 us -> 127 us
  starting transfers between devices: 101 us -> 0 us
  matrix products: 22.3 us -> 0 us
  between operations: 15.3 us -> 0.75 us
  local copies, waits for them, and re-layouts: 15.7 us -> 7.52 us
    psum x1 -> x0, waiting for transfers between devices: 244 us -> none  [settle(): return lax.psum((first_grad, second_grad), ('lon', 'lat'))]
    pallas_call x0 -> x1, Pallas kernels: none -> 127 us  [local(): pl.pallas_call(body, name='backward', out_shape=(jax.ShapeDtypeStruct((T,...]
    ppermute x32 -> x0, waiting for transfers between devices: 103 us -> none  [the longest x16 67.5 us: with_halo(): lax.ppermute(lax.slice_in_dim(block, block.shape[dim] - width, None, axis...]
    ppermute x32 -> x0, starting transfers between devices: 101 us -> none  [the longest x16 67 us: with_halo(): lax.ppermute(lax.slice_in_dim(block, 0, width, axis=dim), axis, backward)]
    dot_general x48 -> x0, matrix products: 22.3 us -> none  [the longest x36 12.7 us: weight_grad(): lax.dot_general(window(widened, row_tap, col_tap, dilation, height, bread...]
    unnamed x42 -> x11, local copies, waits for them, and re-layouts: 12.3 us -> 2.9 us
  transfers between devices with their start and end apart: 33 -> 0, of which waited for: 19 -> 0; matrix products, arithmetic and copies ran while one was open for 6% -> 0% of each run, Pallas kernels for 0% -> 0%
where the time goes in v1:
time: 140 us; the launch traced here: 139 us
  Pallas kernels  127 us (91%)
  local copies, waits for them, and re-layouts  7.52 us (5%)
  other arithmetic  4.43 us (3%)
    pallas_call x1, Pallas kernels, local(): pl.pallas_call(body, name='backward', out_shape=(jax.ShapeDtypeStruct((T,...  127 us
    convert_element_type x2, other arithmetic, unpack(): return jnp.concatenate([taps[:, :C], rest], axis=-1).astype(F32)  4.43 us
    unnamed x11, local copies, waits for them, and re-layouts  2.9 us

profile of v1, /device:TPU:1, one launch (start us, length us, event | category | flops | bytes accessed | tf_op | source)
XLA Modules:
  0.0 139.4 jit_solution(16914248812485049895)
XLA Ops:
  0.6 126.7 %backward.1 = (bf16[32,32,192]{2,1,0:T(8,128)(2,1)}, bf16[3072,128]{1,0:T(8,128)(2,1)}, bf16[3072,128]{1,0:T(8,128)(2,1)}, bf16[3072,128]{1,0:T(8,128)(2,1)}, bf16[3072,128]{1,0:T(8,128)(2,1)}) custom-call(bf16[32,32,192]{2,1,0:T(8,128)(2,1)} %x1.1, bf16[32,32,192]{2,1,0:T(8,128)(2,1)} %a1.1, bf16[32,32,192]{2,1,0:T(8,128)(2,1)} %x2.1, ...), custom_call_target="tpu_custom_call" | custom-call | tf_op jit(solution)/shard_map/backward/pallas_call | solution.py:634
  127.4 0.0 copy-start.1
  127.4 1.2 slice.36
  128.7 0.2 copy.42
  128.9 0.3 copy.34
  129.2 0.0 copy-done.1
  129.2 0.0 copy-start
  129.3 0.2 copy.43
  129.5 0.3 copy.35
  129.8 0.5 copy-done
  130.4 0.2 copy.44
  130.6 0.3 copy.36
  130.9 1.1 slice.45
  132.1 0.9 copy.45
  133.0 1.2 copy.37
  134.2 2.2 %maximum_convert_fusion.2 = (f32[9,192,192]{2,1,0:T(8,128)}, f32[9,192,192]{2,1,0:T(8,128)}) fusion(bf16[9,192,64]{2,1,0:T(8,128)(2,1)S(1)} %bitcast.30, bf16[9,192,128]{2,1,0:T(8,128)(2,1)S(1)} %slice.52, bf16[9,192,64]{2,1,0:T(8,128)(2,1)S(1)} %bitcast.31, bf16[9,192,128]{2,1,0:T(8,128)(2,1)S(1)} %slice.54), kind=kLoop, calls=%fused_computation.2 | loop fusion | flops 2654208 | bytes 3981312 | tf_op jit(solution)/shard_map/convert_element_type | solution.py:627
  136.4 0.0 copy-start.2
  136.4 2.2 %maximum_convert_fusion = (f32[9,192,192]{2,1,0:T(8,128)}, f32[9,192,192]{2,1,0:T(8,128)}) fusion(bf16[9,192,64]{2,1,0:T(8,128)(2,1)S(1)} %bitcast.28, bf16[9,192,128]{2,1,0:T(8,128)(2,1)S(1)} %slice.48, bf16[9,192,64]{2,1,0:T(8,128)(2,1)S(1)} %bitcast.29, bf16[9,192,128]{2,1,0:T(8,128)(2,1)S(1)} %slice.50), kind=kLoop, calls=%fused_computation | loop fusion | flops 2654208 | bytes 3981312 | tf_op jit(solution)/shard_map/convert_element_type | solution.py:627
  138.6 0.0 copy-done.2
  138.7 0.8 copy.47
  (10 shorter events, 0.3 us)
Async XLA Ops:
  127.4 1.8 %copy-start.1 = (bf16[3072,128]{1,0:T(8,128)(2,1)S(1)}, bf16[3072,128]{1,0:T(8,128)(2,1)}, u32[]{:S(2)}) copy-start(bf16[3072,128]{1,0:T(8,128)(2,1)} %get-tuple-element.12) | copy-start | bytes 2359300
  129.2 1.1 copy-start
  136.4 2.2 %copy-start.2 = (bf16[32,32,192]{2,1,0:T(8,128)(2,1)S(1)}, bf16[32,32,192]{2,1,0:T(8,128)(2,1)}, u32[]{:S(2)}) copy-start(bf16[32,32,192]{2,1,0:T(8,128)(2,1)} %get-tuple-element.24) | copy-start | bytes 1179652

commit v2 on v1

--- a/solution.py
+++ b/solution.py
@@ -13,7 +13,7 @@
 F32 = jnp.float32
 T = 32
 ROWS = 3072
-HALF, QUART, SHARD = ROWS // 2, ROWS // 8, ROWS // 32
+HALF, QUART, SHARD = ROWS // 2, ROWS // 8, ROWS // 64
 
 
 class Place:
@@ -29,6 +29,33 @@
         self.south = {"lon": lon, "lat": jnp.maximum(lat - 1, 0)}
         self.twin = {"lon": lon, "lat": lat + 1 - 2 * self.core}
         self.has_north, self.has_south = lat < 3, lat > 0
+        self.ends = (self.z == 0) | (self.z == 7)
+        self.inner = (lat == 1) | (lat == 2)
+        top = (self.z == 7).astype(jnp.int32)
+        half = 1 - top
+        self.here = self.yh == half
+        away = 2 * top - 1
+        beside = (self.x + 4 + away) % 4
+        self.column = jnp.where(self.here, self.x, beside)
+        self.senders = (self.x * 16 + half * 8 + self.z, ((self.x + 4 - away) % 4) * 16 + top * 8 + self.z)
+
+    def column_first(self, to_senders, to_column):
+        @pl.when(self.ends & self.inner)
+        def _():
+            for k, lon in enumerate(self.senders):
+                for lat in range(4):
+                    other = jnp.logical_not(self.here & (self.lat == lat)) if k == 0 else self.ends
+                    pl.when(other)(lambda lon=lon, lat=lat: to_senders({"lon": lon, "lat": lat}))
+
+        if to_column is not None:
+
+            @pl.when(self.ends)
+            def _():
+                for yh in range(2):
+                    for lat in (1, 2):
+                        other = jnp.logical_not(self.here & (self.yh == yh) & (self.lat == lat))
+                        lon = self.column * 16 + yh * 8 + self.z
+                        pl.when(other)(lambda lon=lon, lat=lat: to_column({"lon": lon, "lat": lat}))
 
     def at_x(self, k):
         x = (self.x + k) % 4
@@ -36,8 +63,7 @@
 
     def at_y(self, k):
         y = (self.y + k) % 4
-        lon = self.x * 16 + (y // 2) * 8 + self.z
-        return y, {"lon": lon, "lat": (y % 2) * 2 + self.core}
+        return y, {"lon": self.x * 16 + (y // 2) * 8 + self.z, "lat": (y % 2) * 2 + self.core}
 
     def at_z(self, k):
         z = (self.z + k) % 8
@@ -61,32 +87,31 @@
 
 
 class Reduction:
-    def __init__(self, place, sems, local, from_twin, xs, xr, ys, yr, zs, zr, out):
+    def __init__(self, place, sems, local, from_twin, xs, xr, zs, zr, yr, out):
         self.p, self.local, self.from_twin = place, local, from_twin
-        self.xs, self.xr, self.ys, self.yr, self.zs, self.zr, self.out = xs, xr, ys, yr, zs, zr, out
+        self.xs, self.xr, self.zs, self.zr, self.yr, self.out = xs, xr, zs, zr, yr, out
         p = place
+        self.mine = pl.multiple_of(p.core * HALF, HALF)
         other = pl.multiple_of((1 - p.core) * HALF, HALF)
-        mine = pl.multiple_of(p.core * HALF, HALF)
-        xo = pl.multiple_of(mine + p.x * QUART, QUART)
-        yo = pl.multiple_of(xo + p.y * SHARD, SHARD)
-        self.mine, self.xo, self.yo = mine, xo, yo
+        quarter = pl.multiple_of(self.mine + p.x * QUART, QUART)
+        self.shard = pl.ds(pl.multiple_of(quarter + p.z * SHARD, SHARD), SHARD)
         self.twin = [remote(local.at[pl.ds(other, HALF)], from_twin, *sems.take(), p.twin)]
         self.to_x = []
-        for k in (1, 2, 3):
+        for k in range(1, 4):
             x, where = p.at_x(k)
             src = xs.at[pl.ds(pl.multiple_of(x * QUART, QUART), QUART)]
             self.to_x.append(remote(src, xr.at[k - 1], *sems.take(), where))
-        self.to_y = []
-        for k in (1, 2, 3):
-            y, where = p.at_y(k)
-            src = ys.at[pl.ds(pl.multiple_of(y * SHARD, SHARD), SHARD)]
-            self.to_y.append(remote(src, yr.at[k - 1], *sems.take(), where))
-        self.to_z = [remote(zs, zr.at[p.z], *sems.take(), p.at_z(k)[1]) for k in range(1, 8)]
-        ref = out.at[pl.ds(yo, SHARD)]
-        self.all_y = [remote(ref, ref, *sems.take(), p.at_y(k)[1]) for k in (1, 2, 3)]
-        ref = out.at[pl.ds(xo, QUART)]
-        self.all_x = [remote(ref, ref, *sems.take(), p.at_x(k)[1]) for k in (1, 2, 3)]
-        ref = out.at[pl.ds(mine, HALF)]
+        self.to_z = []
+        for k in range(1, 8):
+            z, where = p.at_z(k)
+            src = zs.at[pl.ds(pl.multiple_of(z * SHARD, SHARD), SHARD)]
+            self.to_z.append(remote(src, zr.at[k - 1], *sems.take(), where))
+        self.to_y = [remote(yr.at[p.y], yr.at[p.y], *sems.take(), p.at_y(k)[1]) for k in range(1, 4)]
+        ref = out.at[self.shard]
+        self.all_z = [remote(ref, ref, *sems.take(), p.at_z(k)[1]) for k in range(1, 8)]
+        ref = out.at[pl.ds(quarter, QUART)]
+        self.all_x = [remote(ref, ref, *sems.take(), p.at_x(k)[1]) for k in range(1, 4)]
+        ref = out.at[pl.ds(self.mine, HALF)]
         self.all_twin = [remote(ref, ref, *sems.take(), p.twin)]
         self.step = 0
 
@@ -118,33 +143,27 @@
 
     def step2(self):
         self.arrive(self.to_x)
-        base = pl.multiple_of(self.p.x * QUART, QUART)
-        total = self.xs[pl.ds(base, QUART)].astype(F32)
+        total = self.xs[pl.ds(pl.multiple_of(self.p.x * QUART, QUART), QUART)].astype(F32)
         for k in range(3):
             total = total + self.xr[k].astype(F32)
-        self.ys[...] = total
+        self.zs[...] = total.astype(BF)
+        self.start(self.to_z)
+
+    def step3(self):
+        self.arrive(self.to_z)
+        total = self.zs[pl.ds(pl.multiple_of(self.p.z * SHARD, SHARD), SHARD)].astype(F32)
+        for k in range(7):
+            total = total + self.zr[k].astype(F32)
+        self.yr[self.p.y] = total
         self.start(self.to_y)
 
-    def step3(self):
+    def step4(self):
         self.arrive(self.to_y)
-        total = self.ys[pl.ds(pl.multiple_of(self.p.y * SHARD, SHARD), SHARD)]
-        for k in range(3):
-            total = total + self.yr[k]
-        total = total.astype(BF)
-        self.zs[...] = total
-        self.zr[self.p.z] = total
-        self.start(self.to_z)
-
-    def step4(self):
-        self.arrive(self.to_z)
-        total = self.zr[0].astype(F32)
-        for k in range(1, 8):
-            total = total + self.zr[k].astype(F32)
-        self.out[pl.ds(self.yo, SHARD)] = total.astype(BF)
-        self.start(self.all_y)
+        self.out[self.shard] = ((self.yr[0] + self.yr[1]) + (self.yr[2] + self.yr[3])).astype(BF)
+        self.start(self.all_z)
 
     def step5(self):
-        self.arrive(self.all_y)
+        self.arrive(self.all_z)
         self.start(self.all_x)
 
     def step6(self):
@@ -155,7 +174,7 @@
         self.arrive(self.all_twin)
 
     def drain(self):
-        for copies in (self.twin, self.to_x, self.to_y, self.to_z, self.all_y, self.all_x, self.all_twin):
+        for copies in (self.twin, self.to_x, self.to_z, self.to_y, self.all_z, self.all_x, self.all_twin):
             for copy in copies:
                 copy.wait_send()
 
@@ -166,6 +185,7 @@
 
 class LonHalo:
     def __init__(self, place, sems, tile, packed, plus, minus, got_plus, got_minus, d):
+        self.p = place
         self.tile, self.packed, self.plus, self.minus, self.d = tile, packed, plus, minus, d
         self.got_plus, self.got_minus = got_plus, got_minus
         low, high = pl.ds(0, d), pl.ds(T - d, d)
@@ -177,16 +197,33 @@
             remote(packed.at[:, low], got_minus, *sems.take(), place.west),
         ]
 
-    def start(self):
-        for copy in self.copies[:2]:
-            copy.start()
+    def start(self, turn=None):
+        p = self.p
+        late = [(p.z == z) if turn is not None else None for z in (7, 0, 7, 0)]
+
+        def go(k):
+            if late[k] is None:
+                self.copies[k].start()
+            else:
+                pl.when(jnp.logical_not(late[k]))(self.copies[k].start)
+
+        go(0)
+        go(1)
         self.packed[...] = pack_rows(self.tile[...], T // 2)
-        for copy in self.copies[2:]:
-            copy.start()
+        go(2)
+        go(3)
         d = self.d
         if d < T:
             self.plus[:, d:, :] = self.tile[:, : T - d, :]
             self.minus[:, : T - d, :] = self.tile[:, d:, :]
+        if turn is not None:
+
+            @pl.when(p.ends)
+            def _():
+                pl.semaphore_wait(turn, 4 - (p.inner & p.here).astype(jnp.int32))
+
+            for k in range(4):
+                pl.when(late[k])(self.copies[k].start)
 
     def arrive(self):
         for copy in self.copies:
@@ -211,12 +248,19 @@
         self.p, self.to_north, self.to_south = place, copies_north, copies_south
 
     def start(self):
+        lat = self.p.lat
+
+        @pl.when(lat == 2)
+        def _():
+            for copy in self.to_south:
+                copy.start()
+
         @pl.when(self.p.has_north)
         def _():
             for copy in self.to_north:
                 copy.start()
 
-        @pl.when(self.p.has_south)
+        @pl.when(self.p.has_south & (lat != 2))
         def _():
             for copy in self.to_south:
                 copy.start()
@@ -377,9 +421,15 @@
                 self.total[pl.ds(d + i * 8, 8)] += self.partial(1, i * 8)
                 self.total[pl.ds(i * 8, 8)] += self.partial(-1, d + i * 8)
 
-    def finish(self, use):
+    def finish(self, use, turn=None):
         d = self.d
         self.halo.arrive()
+        self.halo.drain()
+        if turn is not None:
+
+            self.p.column_first(
+                lambda where: pl.semaphore_signal(turn, inc=1, device_id=where, device_id_type=MESH), None
+            )
 
         def got(slot, row):
             w = self.wide_in[slot, pl.ds(row, 8)].astype(F32)
@@ -429,16 +479,16 @@
             shapes[m + "from_twin"] = v((HALF, 128), F32)
             shapes[m + "xs"] = v((HALF, 128), BF)
             shapes[m + "xr"] = v((3, QUART, 128), BF)
-            shapes[m + "ys"] = v((QUART, 128), F32)
-            shapes[m + "yr"] = v((3, SHARD, 128), F32)
-            shapes[m + "zs"] = v((SHARD, 128), BF)
-            shapes[m + "zr"] = v((8, SHARD, 128), BF)
+            shapes[m + "zs"] = v((QUART, 128), BF)
+            shapes[m + "zr"] = v((7, SHARD, 128), BF)
+            shapes[m + "yr"] = v((4, SHARD, 128), F32)
             shapes[m + "out"] = v((ROWS, 128), BF)
     shapes["total"] = v((T, T, C), F32)
     shapes["dx"] = v((T, T, C), BF)
     shapes["load"] = pltpu.SemaphoreType.DMA((9,))
     shapes["store"] = pltpu.SemaphoreType.DMA((5,))
     shapes["send"] = pltpu.SemaphoreType.DMA((160,))
+    shapes["turn"] = pltpu.SemaphoreType.REGULAR((3,))
     shapes["recv"] = pltpu.SemaphoreType.DMA((160,))
     return shapes
 
@@ -469,7 +519,7 @@
 
     barrier = pltpu.get_barrier_semaphore()
     peers = [p.east, p.west, p.twin]
-    peers += [p.at_x(k)[1] for k in (1, 2, 3)] + [p.at_y(k)[1] for k in (1, 2, 3)]
+    peers += [p.at_x(k)[1] for k in range(1, 4)] + [p.at_y(k)[1] for k in range(1, 4)]
     peers += [p.at_z(k)[1] for k in range(1, 8)]
     for where in peers:
         pl.semaphore_signal(barrier, inc=1, device_id=where, device_id_type=MESH)
@@ -479,12 +529,19 @@
         def _():
             pl.semaphore_signal(barrier, inc=1, device_id=where, device_id_type=MESH)
 
+    def greet(where):
+        pl.semaphore_signal(barrier, inc=1, device_id=where, device_id_type=MESH)
+
+    p.column_first(greet, greet)
     expected = len(peers) + p.has_north.astype(jnp.int32) + p.has_south.astype(jnp.int32)
+    mine = (p.here & p.inner).astype(jnp.int32)
+    expected += p.ends.astype(jnp.int32) * (4 - mine)
+    expected += (p.ends & p.inner).astype(jnp.int32) * (8 - p.here.astype(jnp.int32))
 
     sems = Sems(s["send"], s["recv"])
 
     def reduction(m):
-        names = ("local", "from_twin", "xs", "xr", "ys", "yr", "zs", "zr", "out")
+        names = ("local", "from_twin", "xs", "xr", "zs", "zr", "yr", "out")
         return Reduction(p, sems, *(s[m + n] for n in names))
 
     def lon_halo(m, d):
@@ -535,54 +592,55 @@
     halos["g2"].start()
     loads["a2"].wait()
     gate("2", d2)
-    acts["h2"].start()
-    loads["x2"].wait()
-    acts["x2"].start()
     loads["a1"].wait()
     gate("1", d1)
-    acts["h1"].start()
     loads["x1"].wait()
-    acts["x1"].start()
-    acts["h2"].arrive()
+    loads["x2"].wait()
     for name in ("w22", "w12", "w21", "w11"):
         loads[name].wait()
 
+    turns = [s["turn"].at[k] for k in range(3)]
+
+    halos["g2"].drain()
+    acts["h2"].start()
     halos["g2"].arrive()
     pulls["g2"].send()
     pulls["g2"].stay()
+    pulls["g2"].finish(use_pre("2"), turns[0])
+    halos["q2"].start(turns[0])
+    acts["h2"].arrive()
     weight("h2", "g2", "r22")
     red["r22"].go()
-    acts["x2"].arrive()
-    pulls["g2"].finish(use_pre("2"))
-    halos["q2"].start()
-    red["r22"].go()
-    acts["h1"].arrive()
-    acts["x1"].arrive()
-    red["r22"].go()
+    halos["q2"].drain()
+    acts["x2"].start()
 
     halos["q2"].arrive()
     pulls["q2"].send()
     pulls["q2"].stay()
+    red["r22"].go()
+    pulls["q2"].finish(use_x("2", s["g1"]), turns[1])
+    halos["g1"].start(turns[1])
+    acts["x2"].arrive()
     weight("x2", "q2", "r12")
     red["r12"].go()
-    red["r22"].go()
-    pulls["q2"].finish(use_x("2", s["g1"]))
-    halos["g1"].start()
-    red["r12"].go()
+    halos["g1"].drain()
+    acts["x1"].start()
+    acts["h1"].start()
     red["r22"].go()
 
     halos["g1"].arrive()
     pulls["g1"].send()
     pulls["g1"].stay()
+    red["r12"].go()
+    pulls["g1"].finish(use_pre("1"), turns[2])
+    halos["q1"].start(turns[2])
+    acts["h1"].arrive()
     weight("h1", "g1", "r21")
     red["r21"].go()
+    acts["x1"].arrive()
+    red["r22"].go()
     red["r12"].go()
-    red["r22"].go()
-    pulls["g1"].finish(use_pre("1"))
-    halos["q1"].start()
     red["r21"].go()
-    red["r12"].go()
-    red["r22"].go()
 
     halos["q1"].arrive()
     weight("x1", "q1", "r11")
@@ -590,41 +648,71 @@
     pulls["q1"].send()
     pulls["q1"].stay()
     red["r11"].go()
+    red["r22"].go()
+    red["r12"].go()
     red["r21"].go()
-    red["r12"].go()
     pulls["q1"].finish(use_x("1", s["dx"]))
     stores = [pltpu.make_async_copy(s["dx"], dx_out, s["store"].at[0])]
     stores[0].start()
+    red["r11"].go()
+    red["r12"].go()
     red["r22"].go()
+    red["r21"].go()
     red["r11"].go()
+    red["r12"].go()
+    red["r22"].go()
     red["r21"].go()
+    red["r11"].go()
     red["r12"].go()
+    red["r21"].go()
     red["r11"].go()
-    red["r21"].go()
     red["r12"].go()
-    red["r11"].go()
-    red["r21"].go()
-    red["r12"].go()
-    red["r11"].go()
     red["r21"].go()
     red["r11"].go()
     red["r21"].go()
+    red["r22"].go()
     red["r11"].go()
     for k, (m, out) in enumerate((("r22", r22_out), ("r12", r12_out), ("r21", r21_out), ("r11", r11_out))):
         stores.append(pltpu.make_async_copy(s[m + "out"], out, s["store"].at[1 + k]))
         stores[-1].start()
-    for part in (*halos.values(), *red.values()):
+    halos["q1"].drain()
+    assert all(part.step == 8 for part in red.values())
+    for part in red.values():
         part.drain()
-    for part in (*pulls.values(), *acts.values()):
+    for part in acts.values():
         part.halo.drain()
     for copy in stores:
         copy.wait()
 
 
-def unpack(packed):
-    taps = packed[: 9 * 288].reshape(9, 288, 128)
-    rest = taps[:, C:].reshape(9, C // 2, 2, 64).transpose(0, 2, 1, 3).reshape(9, C, 64)
-    return jnp.concatenate([taps[:, :C], rest], axis=-1).astype(F32)
+def unpack(*refs):
+    tile_in, *sums_in = refs[:5]
+    tile_out, *sums_out = refs[5:10]
+    tile, *buffers = refs[10:19]
+    took, gave = refs[19:]
+    reads = [pltpu.make_async_copy(a, b, took.at[k]) for k, (a, b) in enumerate(zip(sums_in, buffers[:4]))]
+    reads.append(pltpu.make_async_copy(tile_in, tile, took.at[4]))
+    writes = [pltpu.make_async_copy(a, b, gave.at[k]) for k, (a, b) in enumerate(zip(buffers[4:], sums_out))]
+    writes.append(pltpu.make_async_copy(tile, tile_out, gave.at[4]))
+    for copy in reads:
+        copy.start()
+    for k in range(4):
+        reads[k].wait()
+
+        @pl.loop(0, 9)
+        def _(tap):
+            base = pl.multiple_of(tap * 288, 32)
+            wide = buffers[k][pl.ds(base, C)].astype(F32)
+            rest = buffers[k][pl.ds(base + C, C // 2)].astype(F32)
+            buffers[4 + k][tap, :, :128] = wide
+            buffers[4 + k][tap, : C // 2, 128:] = rest[:, :64]
+            buffers[4 + k][tap, C // 2 :, 128:] = rest[:, 64:]
+
+        writes[k].start()
+    reads[4].wait()
+    writes[4].start()
+    for copy in writes:
+        copy.wait()
 
 
 def local(x1, a1, x2, a2, g2, w11, w21, w12, w22):
@@ -642,7 +730,18 @@
             collective_id=0, has_side_effects=True, vmem_limit_bytes=60 * 1024 * 1024
         ),
     )(x1, a1, x2, a2, g2, w11, w21, w12, w22)
-    return (dx, *(unpack(v) for v in sums))
+    full = jax.ShapeDtypeStruct((9, C, C), F32)
+    return pl.pallas_call(
+        unpack,
+        name="unpack",
+        out_shape=(jax.ShapeDtypeStruct((T, T, C), BF), full, full, full, full),
+        in_specs=[anywhere] * 5,
+        out_specs=[anywhere] * 5,
+        scratch_shapes=[pltpu.VMEM((T, T, C), BF)]
+        + [pltpu.VMEM((ROWS, 128), BF)] * 4
+        + [pltpu.VMEM((9, C, C), F32)] * 4
+        + [pltpu.SemaphoreType.DMA((5,)), pltpu.SemaphoreType.DMA((5,))],
+    )(dx, *sums)
 
 
 def solution(mesh):

time: 140 us -> 128 us (0.914)
  local copies, waits for them, and re-layouts: 7.52 us -> 0 us
  other arithmetic: 4.43 us -> 0 us
    pallas_call x0 -> x1, Pallas kernels: none -> 5.42 us  [local(): pl.pallas_call(unpack, name='unpack', out_shape=(jax.ShapeDtypeStruct((T,...]
    pallas_call x1, Pallas kernels: 127 us -> 122 us  [local(): pl.pallas_call(body, name='backward', out_shape=(jax.ShapeDtypeStruct((T,...]
    convert_element_type x2 -> x0, other arithmetic: 4.43 us -> none  [unpack(): return jnp.concatenate([taps[:, :C], rest], axis=-1).astype(F32)]
    unnamed x11 -> x0, local copies, waits for them, and re-layouts: 2.9 us -> none
    slice x12 -> x0, local copies, waits for them, and re-layouts: 2.62 us -> none  [the longest x4 2.44 us: unpack(): taps = packed[:9 * 288].reshape(9, 288, 128)]
    reshape x4 -> x0, local copies, waits for them, and re-layouts: 2 us -> none  [unpack(): taps[:, C:].reshape(9, C // 2, 2, 64).transpose(0, 2, 1, 3)]
where the time goes in v2:
time: 128 us
  Pallas kernels  127 us (99%)
    pallas_call x1, Pallas kernels, local(): pl.pallas_call(body, name='backward', out_shape=(jax.ShapeDtypeStruct((T,...  122 us
    pallas_call x1, Pallas kernels, local(): pl.pallas_call(unpack, name='unpack', out_shape=(jax.ShapeDtypeStruct((T,...  5.42 us

profile of v2, /device:TPU:1, one launch (start us, length us, event | category | flops | bytes accessed | tf_op | source)
XLA Modules:
  0.0 127.7 jit_solution(12567147908186474518)
XLA Ops:
  0.6 121.7 %backward.1 = (bf16[32,32,192]{2,1,0:T(8,128)(2,1)}, bf16[3072,128]{1,0:T(8,128)(2,1)}, bf16[3072,128]{1,0:T(8,128)(2,1)}, bf16[3072,128]{1,0:T(8,128)(2,1)}, bf16[3072,128]{1,0:T(8,128)(2,1)}) custom-call(bf16[32,32,192]{2,1,0:T(8,128)(2,1)} %x1.1, bf16[32,32,192]{2,1,0:T(8,128)(2,1)} %a1.1, bf16[32,32,192]{2,1,0:T(8,128)(2,1)} %x2.1, ...), custom_call_target="tpu_custom_call" | custom-call | tf_op jit(solution)/shard_map/backward/pallas_call | solution.py:722
  122.3 5.4 %unpack.1 = (bf16[32,32,192]{2,1,0:T(8,128)(2,1)}, f32[9,192,192]{2,1,0:T(8,128)}, f32[9,192,192]{2,1,0:T(8,128)}, f32[9,192,192]{2,1,0:T(8,128)}, f32[9,192,192]{2,1,0:T(8,128)}) custom-call(bf16[32,32,192]{2,1,0:T(8,128)(2,1)} %get-tuple-element.10.refs_0_, bf16[3072,128]{1,0:T(8,128)(2,1)} %get-tuple-element.11.refs_1_, ...), custom_call_target="tpu_custom_call" | custom-call | tf_op jit(solution)/shard_map/unpack/pallas_call | solution.py:734

commit v3 on v2

--- a/solution.py
+++ b/solution.py
@@ -13,7 +13,7 @@
 F32 = jnp.float32
 T = 32
 ROWS = 3072
-HALF, QUART, SHARD = ROWS // 2, ROWS // 8, ROWS // 64
+HALF, QUART, PART, SHARD = ROWS // 2, ROWS // 8, ROWS // 32, ROWS // 64
 
 
 class Place:
@@ -65,6 +65,10 @@
         y = (self.y + k) % 4
         return y, {"lon": self.x * 16 + (y // 2) * 8 + self.z, "lat": (y % 2) * 2 + self.core}
 
+    def at_xy(self, k):
+        x, y = (self.x + k // 4) % 4, (self.y + k % 4) % 4
+        return x * 4 + y, {"lon": x * 16 + (y // 2) * 8 + self.z, "lat": (y % 2) * 2 + self.core}
+
     def at_z(self, k):
         z = (self.z + k) % 8
         return z, {"lon": self.lon - self.z + z, "lat": self.lat}
@@ -87,18 +91,21 @@
 
 
 class Reduction:
-    def __init__(self, place, sems, local, from_twin, xs, xr, zs, zr, yr, out):
+    def __init__(self, place, sems, along_x, local, from_twin, xs, xr, zs, zr, yr, out):
         self.p, self.local, self.from_twin = place, local, from_twin
         self.xs, self.xr, self.zs, self.zr, self.yr, self.out = xs, xr, zs, zr, yr, out
         p = place
+        self.wide, at_wide = (p.x, p.at_x) if along_x else (p.y, p.at_y)
+        thin, at_thin = (p.y, p.at_y) if along_x else (p.x, p.at_x)
+        self.thin = thin
         self.mine = pl.multiple_of(p.core * HALF, HALF)
         other = pl.multiple_of((1 - p.core) * HALF, HALF)
-        quarter = pl.multiple_of(self.mine + p.x * QUART, QUART)
+        quarter = pl.multiple_of(self.mine + self.wide * QUART, QUART)
         self.shard = pl.ds(pl.multiple_of(quarter + p.z * SHARD, SHARD), SHARD)
         self.twin = [remote(local.at[pl.ds(other, HALF)], from_twin, *sems.take(), p.twin)]
         self.to_x = []
         for k in range(1, 4):
-            x, where = p.at_x(k)
+            x, where = at_wide(k)
             src = xs.at[pl.ds(pl.multiple_of(x * QUART, QUART), QUART)]
             self.to_x.append(remote(src, xr.at[k - 1], *sems.take(), where))
         self.to_z = []
@@ -106,13 +113,15 @@
             z, where = p.at_z(k)
             src = zs.at[pl.ds(pl.multiple_of(z * SHARD, SHARD), SHARD)]
             self.to_z.append(remote(src, zr.at[k - 1], *sems.take(), where))
-        self.to_y = [remote(yr.at[p.y], yr.at[p.y], *sems.take(), p.at_y(k)[1]) for k in range(1, 4)]
+        self.to_y = [remote(yr.at[thin], yr.at[thin], *sems.take(), at_thin(k)[1]) for k in range(1, 4)]
         ref = out.at[self.shard]
         self.all_z = [remote(ref, ref, *sems.take(), p.at_z(k)[1]) for k in range(1, 8)]
         ref = out.at[pl.ds(quarter, QUART)]
-        self.all_x = [remote(ref, ref, *sems.take(), p.at_x(k)[1]) for k in range(1, 4)]
-        ref = out.at[pl.ds(self.mine, HALF)]
-        self.all_twin = [remote(ref, ref, *sems.take(), p.twin)]
+        self.all_x = [remote(ref, ref, *sems.take(), at_wide(k)[1]) for k in range(1, 4)]
+        self.all_twin = []
+        for k in range(4):
+            ref = out.at[pl.ds(pl.multiple_of(self.mine + ((self.wide + 4 - k) % 4) * QUART, QUART), QUART)]
+            self.all_twin.append(remote(ref, ref, *sems.take(), p.twin))
         self.step = 0
 
     def go(self):
@@ -143,7 +152,7 @@
 
     def step2(self):
         self.arrive(self.to_x)
-        total = self.xs[pl.ds(pl.multiple_of(self.p.x * QUART, QUART), QUART)].astype(F32)
+        total = self.xs[pl.ds(pl.multiple_of(self.wide * QUART, QUART), QUART)].astype(F32)
         for k in range(3):
             total = total + self.xr[k].astype(F32)
         self.zs[...] = total.astype(BF)
@@ -154,7 +163,7 @@
         total = self.zs[pl.ds(pl.multiple_of(self.p.z * SHARD, SHARD), SHARD)].astype(F32)
         for k in range(7):
             total = total + self.zr[k].astype(F32)
-        self.yr[self.p.y] = total
+        self.yr[self.thin] = total
         self.start(self.to_y)
 
     def step4(self):
@@ -165,10 +174,12 @@
     def step5(self):
         self.arrive(self.all_z)
         self.start(self.all_x)
+        self.all_twin[0].start()
 
     def step6(self):
-        self.arrive(self.all_x)
-        self.start(self.all_twin)
+        for k in range(3):
+            self.all_x[k].wait_recv()
+            self.all_twin[k + 1].start()
 
     def step7(self):
         self.arrive(self.all_twin)
@@ -177,6 +188,56 @@
         for copies in (self.twin, self.to_x, self.to_z, self.to_y, self.all_z, self.all_x, self.all_twin):
             for copy in copies:
                 copy.wait_send()
+
+
+class LastReduction(Reduction):
+    def __init__(self, place, sems, local, from_twin, xs, xr, zs, zr, out):
+        self.p, self.local, self.from_twin = place, local, from_twin
+        self.xs, self.xr, self.zs, self.zr, self.out = xs, xr, zs, zr, out
+        p = place
+        self.mine = pl.multiple_of(p.core * HALF, HALF)
+        other = pl.multiple_of((1 - p.core) * HALF, HALF)
+        self.own = pl.multiple_of((p.x * 4 + p.y) * PART, PART)
+        self.twin = [remote(local.at[pl.ds(other, HALF)], from_twin, *sems.take(), p.twin)]
+        self.to_x = []
+        for k in range(1, 16):
+            xy, where = p.at_xy(k)
+            src = xs.at[pl.ds(pl.multiple_of(xy * PART, PART), PART)]
+            self.to_x.append(remote(src, xr.at[k - 1], *sems.take(), where))
+        self.to_z = [remote(zs, zr.at[p.z], *sems.take(), p.at_z(k)[1]) for k in range(1, 8)]
+        self.to_y = []
+        self.shard = pl.ds(pl.multiple_of(self.mine + self.own, PART), PART)
+        ref = out.at[self.shard]
+        self.all_z = [remote(ref, ref, *sems.take(), p.at_xy(k)[1]) for k in range(1, 16)]
+        self.all_x = []
+        ref = out.at[pl.ds(self.mine, HALF)]
+        self.all_twin = [remote(ref, ref, *sems.take(), p.twin)]
+        self.step = 0
+
+    def step2(self):
+        self.arrive(self.to_x)
+        total = self.xs[pl.ds(self.own, PART)].astype(F32)
+        for k in range(15):
+            total = total + self.xr[k].astype(F32)
+        total = total.astype(BF)
+        self.zs[...] = total
+        self.zr[self.p.z] = total
+        self.start(self.to_z)
+
+    def step3(self):
+        self.arrive(self.to_z)
+        total = self.zr[0].astype(F32)
+        for k in range(1, 8):
+            total = total + self.zr[k].astype(F32)
+        self.out[self.shard] = total.astype(BF)
+        self.start(self.all_z)
+
+    def step4(self):
+        self.arrive(self.all_z)
+        self.start(self.all_twin)
+
+    def step5(self):
+        self.arrive(self.all_twin)
 
 
 def pack_rows(v, half):
@@ -342,20 +403,18 @@
             v = self.wide[pl.ds(i * 8, 8)].reshape(8 * T, C)
             self.turned[:, pl.ds(pl.multiple_of(i * 8 * T, 8 * T), 8 * T)] = v.T
 
-    def weight_gradient(self, minus, tile, plus, into):
+    def weight_gradient(self, gradients, into):
         cells = T * T
 
         @pl.loop(0, 3)
         def _(r):
             start = pl.multiple_of(r * self.d * T, 512)
             turned = self.turned[:, pl.ds(start, cells)]
-            for c, g in enumerate((minus, tile, plus)):
+            for c, g in gradients:
                 d = jnp.dot(turned, g[...].reshape(cells, C), preferred_element_type=F32)
                 base = pl.multiple_of((3 * r + c) * 288, 32)
                 into[pl.ds(base, C)] = d[:, :128]
                 into[pl.ds(base + C, C // 2)] = jnp.concatenate([d[: C // 2, 128:], d[C // 2 :, 128:]], axis=1)
-
-        into[9 * 288 :] = jnp.zeros((ROWS - 9 * 288, 128), F32)
 
 
 class Pull:
@@ -375,27 +434,33 @@
             ],
         )
 
-    def partial(self, r, row):
+    def partial(self, r, row, rows=8):
         total = None
         for c in range(3):
-            g = self.g[c][pl.ds(row, 8)].reshape(8 * T, C)
+            g = self.g[c][pl.ds(row, rows)].reshape(rows * T, C)
             term = lax.dot_general(
                 g, self.w[3 * (r + 1) + c], (((1,), (1,)), ((), ())), preferred_element_type=F32
             )
             total = term if total is None else total + term
-        return total.reshape(8, T, C)
+        return total.reshape(rows, T, C)
 
     def send(self):
-        d = self.d
-
-        @pl.loop(0, d // 8)
-        def _(i):
-            for slot, r, first in ((0, 1, T - d), (1, -1, 0)):
-                v = self.partial(r, first + i * 8).astype(BF)
-                self.wide_out[slot, pl.ds(i * 8, 8)] = v[:, :, :128]
-                self.packed_out[slot, pl.ds(i * 8, 8)] = pack_columns(v)
-
-        self.halo.start()
+        d, p = self.d, self.p
+        slots = ((p.has_north, 1, T - d, self.halo.to_north), (p.has_south, -1, 0, self.halo.to_south))
+        for core, order in ((1, (0, 1)), (0, (1, 0))):
+            for slot in order:
+                there, r, first, copies = slots[slot]
+
+                @pl.when((p.core == core) & there)
+                def _(slot=slot, r=r, first=first, copies=copies):
+                    @pl.loop(0, d // 16)
+                    def _(i):
+                        v = self.partial(r, first + i * 16, 16).astype(BF)
+                        self.wide_out[slot, pl.ds(i * 16, 16)] = v[:, :, :128]
+                        self.packed_out[slot, pl.ds(i * 16, 16)] = pack_columns(v)
+
+                    for copy in copies:
+                        copy.start()
 
         @pl.when(jnp.logical_not(self.p.has_south))
         def _():
@@ -423,13 +488,13 @@
 
     def finish(self, use, turn=None):
         d = self.d
-        self.halo.arrive()
         self.halo.drain()
         if turn is not None:
 
             self.p.column_first(
                 lambda where: pl.semaphore_signal(turn, inc=1, device_id=where, device_id_type=MESH), None
             )
+        self.halo.arrive()
 
         def got(slot, row):
             w = self.wide_in[slot, pl.ds(row, 8)].astype(F32)
@@ -477,19 +542,21 @@
             m = "r" + n + b
             shapes[m + "local"] = v((ROWS, 128), F32)
             shapes[m + "from_twin"] = v((HALF, 128), F32)
+            last = m == "r11"
             shapes[m + "xs"] = v((HALF, 128), BF)
-            shapes[m + "xr"] = v((3, QUART, 128), BF)
-            shapes[m + "zs"] = v((QUART, 128), BF)
-            shapes[m + "zr"] = v((7, SHARD, 128), BF)
-            shapes[m + "yr"] = v((4, SHARD, 128), F32)
+            shapes[m + "xr"] = v((15, PART, 128) if last else (3, QUART, 128), BF)
+            shapes[m + "zs"] = v((PART if last else QUART, 128), BF)
+            shapes[m + "zr"] = v((8, PART, 128) if last else (7, SHARD, 128), BF)
+            if not last:
+                shapes[m + "yr"] = v((4, SHARD, 128), F32)
             shapes[m + "out"] = v((ROWS, 128), BF)
     shapes["total"] = v((T, T, C), F32)
     shapes["dx"] = v((T, T, C), BF)
     shapes["load"] = pltpu.SemaphoreType.DMA((9,))
     shapes["store"] = pltpu.SemaphoreType.DMA((5,))
-    shapes["send"] = pltpu.SemaphoreType.DMA((160,))
+    shapes["send"] = pltpu.SemaphoreType.DMA((192,))
     shapes["turn"] = pltpu.SemaphoreType.REGULAR((3,))
-    shapes["recv"] = pltpu.SemaphoreType.DMA((160,))
+    shapes["recv"] = pltpu.SemaphoreType.DMA((192,))
     return shapes
 
 
@@ -519,7 +586,7 @@
 
     barrier = pltpu.get_barrier_semaphore()
     peers = [p.east, p.west, p.twin]
-    peers += [p.at_x(k)[1] for k in range(1, 4)] + [p.at_y(k)[1] for k in range(1, 4)]
+    peers += [p.at_xy(k)[1] for k in range(1, 16)]
     peers += [p.at_z(k)[1] for k in range(1, 8)]
     for where in peers:
         pl.semaphore_signal(barrier, inc=1, device_id=where, device_id_type=MESH)
@@ -541,8 +608,11 @@
     sems = Sems(s["send"], s["recv"])
 
     def reduction(m):
+        if m == "r11":
+            names = ("local", "from_twin", "xs", "xr", "zs", "zr", "out")
+            return LastReduction(p, sems, *(s[m + n] for n in names))
         names = ("local", "from_twin", "xs", "xr", "zs", "zr", "yr", "out")
-        return Reduction(p, sems, *(s[m + n] for n in names))
+        return Reduction(p, sems, True, *(s[m + n] for n in names))
 
     def lon_halo(m, d):
         names = ("", "packed", "plus", "minus", "got_plus", "got_minus")
@@ -584,9 +654,12 @@
 
         return use
 
-    def weight(act, m, r):
-        acts[act].weight_gradient(s[m + "minus"], s[m], s[m + "plus"], s[r + "local"])
-
+    def weight(act, m, r, columns=(0, 1, 2)):
+        names = (m + "minus", m, m + "plus")
+        acts[act].weight_gradient([(c, s[names[c]]) for c in columns], s[r + "local"])
+
+    for m in red:
+        s[m + "local"][9 * 288 :] = jnp.zeros((ROWS - 9 * 288, 128), F32)
     loads["g2"].wait()
     pl.semaphore_wait(barrier, expected)
     halos["g2"].start()
@@ -613,70 +686,69 @@
     red["r22"].go()
     halos["q2"].drain()
     acts["x2"].start()
+    red["r22"].go()
 
     halos["q2"].arrive()
     pulls["q2"].send()
     pulls["q2"].stay()
-    red["r22"].go()
     pulls["q2"].finish(use_x("2", s["g1"]), turns[1])
     halos["g1"].start(turns[1])
     acts["x2"].arrive()
     weight("x2", "q2", "r12")
     red["r12"].go()
+    red["r22"].go()
     halos["g1"].drain()
     acts["x1"].start()
     acts["h1"].start()
-    red["r22"].go()
+    red["r12"].go()
 
     halos["g1"].arrive()
     pulls["g1"].send()
     pulls["g1"].stay()
-    red["r12"].go()
-    pulls["g1"].finish(use_pre("1"), turns[2])
-    halos["q1"].start(turns[2])
     acts["h1"].arrive()
     weight("h1", "g1", "r21")
     red["r21"].go()
+    red["r22"].go()
+    pulls["g1"].finish(use_pre("1"), turns[2])
+    halos["q1"].start(turns[2])
+    red["r21"].go()
+    red["r12"].go()
+    red["r22"].go()
     acts["x1"].arrive()
+    weight("x1", "q1", "r11", (1,))
     red["r22"].go()
     red["r12"].go()
     red["r21"].go()
 
     halos["q1"].arrive()
-    weight("x1", "q1", "r11")
+    weight("x1", "q1", "r11", (0, 2))
     red["r11"].go()
     pulls["q1"].send()
+    red["r11"].go()
     pulls["q1"].stay()
-    red["r11"].go()
     red["r22"].go()
-    red["r12"].go()
-    red["r21"].go()
-    pulls["q1"].finish(use_x("1", s["dx"]))
-    stores = [pltpu.make_async_copy(s["dx"], dx_out, s["store"].at[0])]
-    stores[0].start()
-    red["r11"].go()
-    red["r12"].go()
-    red["r22"].go()
-    red["r21"].go()
-    red["r11"].go()
-    red["r12"].go()
-    red["r22"].go()
-    red["r21"].go()
-    red["r11"].go()
     red["r12"].go()
     red["r21"].go()
     red["r11"].go()
     red["r12"].go()
     red["r21"].go()
+    red["r22"].go()
     red["r11"].go()
     red["r21"].go()
-    red["r22"].go()
+    pulls["q1"].finish(use_x("1", s["dx"]))
+    stores = [pltpu.make_async_copy(s["dx"], dx_out, s["store"].at[0])]
+    stores[0].start()
+    red["r12"].go()
+    red["r21"].go()
     red["r11"].go()
+    red["r12"].go()
+    red["r11"].go()
+    red["r21"].go()
     for k, (m, out) in enumerate((("r22", r22_out), ("r12", r12_out), ("r21", r21_out), ("r11", r11_out))):
         stores.append(pltpu.make_async_copy(s[m + "out"], out, s["store"].at[1 + k]))
         stores[-1].start()
     halos["q1"].drain()
-    assert all(part.step == 8 for part in red.values())
+    assert [part.step for part in red.values()] == [8, 8, 8, 6]
     for part in red.values():
         part.drain()
     for part in acts.values():

time: 128 us -> 124 us (0.969)
  Pallas kernels: 127 us -> 123 us
    pallas_call x1, Pallas kernels: 122 us -> 118 us  [local(): pl.pallas_call(body, name='backward', out_shape=(jax.ShapeDtypeStruct((T,...]
where the time goes in v3:
time: 124 us
  Pallas kernels  123 us (99%)
    pallas_call x1, Pallas kernels, local(): pl.pallas_call(body, name='backward', out_shape=(jax.ShapeDtypeStruct((T,...  118 us
    pallas_call x1, Pallas kernels, local(): pl.pallas_call(unpack, name='unpack', out_shape=(jax.ShapeDtypeStruct((T,...  5.42 us

profile of v3, /device:TPU:1, one launch (start us, length us, event | category | flops | bytes accessed | tf_op | source)
XLA Modules:
  0.0 123.9 jit_solution(13647851629781996041)
XLA Ops:
  0.6 117.9 %backward.1 = (bf16[32,32,192]{2,1,0:T(8,128)(2,1)}, bf16[3072,128]{1,0:T(8,128)(2,1)}, bf16[3072,128]{1,0:T(8,128)(2,1)}, bf16[3072,128]{1,0:T(8,128)(2,1)}, bf16[3072,128]{1,0:T(8,128)(2,1)}) custom-call(bf16[32,32,192]{2,1,0:T(8,128)(2,1)} %x1.1, bf16[32,32,192]{2,1,0:T(8,128)(2,1)} %a1.1, bf16[32,32,192]{2,1,0:T(8,128)(2,1)} %x2.1, ...), custom_call_target="tpu_custom_call" | custom-call | tf_op jit(solution)/shard_map/backward/pallas_call | solution.py:794
  118.5 5.4 %unpack.1 = (bf16[32,32,192]{2,1,0:T(8,128)(2,1)}, f32[9,192,192]{2,1,0:T(8,128)}, f32[9,192,192]{2,1,0:T(8,128)}, f32[9,192,192]{2,1,0:T(8,128)}, f32[9,192,192]{2,1,0:T(8,128)}) custom-call(bf16[32,32,192]{2,1,0:T(8,128)(2,1)} %get-tuple-element.10.refs_0_, bf16[3072,128]{1,0:T(8,128)(2,1)} %get-tuple-element.11.refs_1_, ...), custom_call_target="tpu_custom_call" | custom-call | tf_op jit(solution)/shard_map/unpack/pallas_call | solution.py:806

commit v4 on v3

--- a/solution.py
+++ b/solution.py
@@ -129,8 +129,16 @@
         self.step += 1
 
     def start(self, copies):
-        for copy in copies:
-            copy.start()
+        size = len(copies) + 1
+
+        def hops(at):
+            k = at + 1
+            if size == 16:
+                return min(k // 4, 4 - k // 4) + min(k % 4, 4 - k % 4)
+            return min(k, size - k)
+
+        for at in sorted(range(len(copies)), key=hops, reverse=True):
+            copies[at].start()
 
     def arrive(self, copies):
         for copy in copies:
@@ -725,16 +733,16 @@
     red["r11"].go()
     pulls["q1"].send()
     red["r11"].go()
-    pulls["q1"].stay()
     red["r22"].go()
     red["r12"].go()
     red["r21"].go()
+    pulls["q1"].stay()
+    red["r21"].go()
+    red["r12"].go()
     red["r11"].go()
-    red["r12"].go()
+    red["r22"].go()
     red["r21"].go()
-    red["r22"].go()
     red["r11"].go()
-    red["r21"].go()
     pulls["q1"].finish(use_x("1", s["dx"]))
     stores = [pltpu.make_async_copy(s["dx"], dx_out, s["store"].at[0])]
     stores[0].start()

time: 124 us -> 121 us (0.976)
  Pallas kernels: 123 us -> 121 us
    pallas_call x1, Pallas kernels: 118 us -> 115 us  [local(): pl.pallas_call(body, name='backward', out_shape=(jax.ShapeDtypeStruct((T,...]
where the time goes in v4:
time: 121 us
  Pallas kernels  121 us (100%)
    pallas_call x1, Pallas kernels, local(): pl.pallas_call(body, name='backward', out_shape=(jax.ShapeDtypeStruct((T,...  115 us
    pallas_call x1, Pallas kernels, local(): pl.pallas_call(unpack, name='unpack', out_shape=(jax.ShapeDtypeStruct((T,...  5.42 us

profile of v4, /device:TPU:1, one launch (start us, length us, event | category | flops | bytes accessed | tf_op | source)
XLA Modules:
  0.0 121.4 jit_solution(12675010480071725207)
XLA Ops:
  0.6 115.3 %backward.1 = (bf16[32,32,192]{2,1,0:T(8,128)(2,1)}, bf16[3072,128]{1,0:T(8,128)(2,1)}, bf16[3072,128]{1,0:T(8,128)(2,1)}, bf16[3072,128]{1,0:T(8,128)(2,1)}, bf16[3072,128]{1,0:T(8,128)(2,1)}) custom-call(bf16[32,32,192]{2,1,0:T(8,128)(2,1)} %x1.1, bf16[32,32,192]{2,1,0:T(8,128)(2,1)} %a1.1, bf16[32,32,192]{2,1,0:T(8,128)(2,1)} %x2.1, ...), custom_call_target="tpu_custom_call" | custom-call | tf_op jit(solution)/shard_map/backward/pallas_call | solution.py:802
  116.0 5.4 %unpack.1 = (bf16[32,32,192]{2,1,0:T(8,128)(2,1)}, f32[9,192,192]{2,1,0:T(8,128)}, f32[9,192,192]{2,1,0:T(8,128)}, f32[9,192,192]{2,1,0:T(8,128)}, f32[9,192,192]{2,1,0:T(8,128)}) custom-call(bf16[32,32,192]{2,1,0:T(8,128)(2,1)} %get-tuple-element.10.refs_0_, bf16[3072,128]{1,0:T(8,128)(2,1)} %get-tuple-element.11.refs_1_, ...), custom_call_target="tpu_custom_call" | custom-call | tf_op jit(solution)/shard_map/unpack/pallas_call | solution.py:814
